TPU v7x, 32 devices: a whole 2x2x4 slice. The times are simulated.
32 devices in a mesh: groups: 2 (over x), rows: 16 (over z, y, core).
Axes of the slice: x: 2, y: 2, z: 4, core: 2. Of those that a mesh axis runs over, the one named last changes fastest.
Arguments:
- token_ids: int32 [1, 256], P(None, 'groups'), parts along dimension 1, may hold values from 0 to 32767
- parents: int32 [1, 8, 32], P(None, 'groups'), parts along dimension 1, may hold values from 0 to 31, as said below
- states: bfloat16 [256, 16, 128, 128], P(('groups', 'rows')), parts along dimension 0, may hold values from -1.75 to 1.75
- embed_table: bfloat16 [32768, 2048], P(None, 'rows'), may hold values from -6 to 6
- qkv_weight: bfloat16 [2048, 3, 2048], P(None, None, 'rows'), may hold values from -0.125 to 0.125
- gate_weight: float32 [16, 128], replicated, may hold values from -6 to 6
- gate_bias: float32 [16], replicated, may hold values from -2 to 3
- norm_gain: float32 [2048], replicated, may hold values from 0.1 to 1.9
- out_weight: bfloat16 [2048, 2048], P(None, 'rows'), may hold values from -0.125 to 0.125
Outputs:
- layer_out: bfloat16 [1, 256, 2048], P(None, 'groups', 'rows'), parts along dimension 1
- final_states: bfloat16 [256, 16, 128, 128], P(('groups', 'rows')), parts along dimension 0
There are 2 independent parts, one for each index of `groups`. A program takes and returns all parts, laid end to end along the dimension named above; an argument that names none is the same for every part. Nothing has to cross between parts.
Inputs may be any that keep to these rules, and one draw needn't show every extreme that they name: The 32 beams of a user fall into 4 aligned blocks of 8. In every step and for every user, at most 2 children of one block have parents in any one other block, and in every step some user has exactly 2 children of one block with parents in another block.
All inputs are finite; a program needn't handle non-finite values.
Results may differ from a plain program's by a relative error of at most 0.0074.
Values may be sent and summed in bfloat16 or wider, within the bound.
A program may use at most 64 MiB of HBM per device.

v0:
```python
import math

import jax
import jax.numpy as jnp
from jax import lax
from jax.sharding import PartitionSpec as P

CAP = 2


def from_partner(block, axis, stride):
    count = lax.axis_size(axis)
    route = []
    for low in range(count):
        high = low | 1 << stride
        if high != low and high < count:
            route += [(low, high), (high, low)]
    return lax.ppermute(block, axis, route)


def outgoing(state_now, parent_list, member, row_local, partner):
    target = jnp.bitwise_xor(member, partner)
    children = lax.dynamic_slice_in_dim(parent_list, target * row_local, row_local, 0)
    needed = children // row_local == member
    rank_index = jnp.cumsum(needed.astype(jnp.int32)) - 1
    slot_ids = jnp.arange(CAP, dtype=jnp.int32)
    chosen = jnp.sum(
        jnp.where(
            needed[None, :] & (rank_index[None, :] == slot_ids[:, None]),
            (children % row_local)[None, :],
            0,
        ),
        axis=1,
    )
    return jnp.take(state_now, chosen, axis=0)


def route(state_now, parent_list, member, row_local):
    first_out = outgoing(state_now, parent_list, member, row_local, 1)
    second_out = outgoing(state_now, parent_list, member, row_local, 2)
    corner_out = outgoing(state_now, parent_list, member, row_local, 3)
    got_one = from_partner(first_out, "rows", 0)
    got_two = from_partner(second_out, "rows", 1)
    relayed = from_partner(corner_out, "rows", 0)
    got_three = from_partner(relayed, "rows", 1)
    own_list = lax.dynamic_slice_in_dim(parent_list, member * row_local, row_local, 0)
    source = own_list // row_local
    partner = jnp.bitwise_xor(source, member)
    slot_index = jnp.arange(row_local, dtype=jnp.int32)
    earlier = (source[:, None] == source[None, :]) & (slot_index[:, None] > slot_index[None, :])
    rank_index = jnp.sum(earlier.astype(jnp.int32), axis=1)
    position = jnp.where(
        partner == 0, own_list % row_local, row_local + (partner - 1) * CAP + rank_index
    )
    pooled = jnp.concatenate([state_now, got_one, got_two, got_three], 0)
    return jnp.take(pooled, position, axis=0)


def per_device(
    token_ids,
    parents,
    states,
    embed_table,
    qkv_weight,
    gate_weight,
    gate_bias,
    norm_gain,
    out_weight,
):
    row_local = states.shape[0]
    heads = states.shape[1]
    head_size = states.shape[2]
    width = heads * head_size
    column_local = embed_table.shape[1]
    row_total = token_ids.shape[1]
    device = lax.axis_index("rows")
    member = device % 4
    user_index = device // 4
    weight_flat = qkv_weight.reshape(qkv_weight.shape[0], 3 * column_local)
    local_columns = jnp.take(embed_table, token_ids, axis=0)
    every_proj = jnp.einsum(
        "...rc,cf->...rf",
        lax.all_gather(local_columns, "rows", axis=2, tiled=True),
        weight_flat,
        preferred_element_type=jnp.float32,
    )
    state_now = states
    step_proj = every_proj[0]
    projected = step_proj.astype(jnp.bfloat16).reshape(row_total, 3, column_local)
    mine = lax.all_to_all(projected, "rows", split_axis=0, concat_axis=2, tiled=True)
    queries = mine[:, 0].reshape(row_local, heads, head_size)
    key_float = mine[:, 1].reshape(row_local, heads, head_size).astype(jnp.float32)
    values = mine[:, 2].reshape(row_local, heads, head_size).astype(jnp.float32)
    gate_logit = jnp.sum(key_float * gate_weight, axis=-1) / math.sqrt(head_size) + gate_bias
    decay_rate = jax.nn.sigmoid(gate_logit)
    key_unit = key_float * lax.rsqrt(jnp.sum(key_float * key_float, axis=-1, keepdims=True) + 1e-06)
    parent_list = lax.dynamic_index_in_dim(parents[0], user_index, 0, keepdims=False)
    prior_state = route(state_now, parent_list, member, row_local)
    new_state = (
        decay_rate[:, :, None, None] * prior_state.astype(jnp.float32)
        + key_unit[:, :, :, None] * values[:, :, None, :]
    )
    state_now = new_state.astype(jnp.bfloat16)
    readout = jnp.einsum("rhd,rhde->rhe", queries, state_now, preferred_element_type=jnp.float32)
    scaled = readout * lax.rsqrt(jnp.mean(readout * readout, axis=-1, keepdims=True) + 1e-05)
    normed = (scaled.reshape(row_local, width) * norm_gain).astype(jnp.bfloat16)
    attention = jnp.dot(
        lax.all_gather(normed, "rows", axis=0, tiled=True),
        out_weight,
        preferred_element_type=jnp.float32,
    )
    outputs = [(local_columns[0].astype(jnp.float32) + attention).astype(jnp.bfloat16)]
    return (jnp.stack(outputs), state_now)


def solution(mesh):
    placed = (
        P(None, "groups"),
        P(None, "groups", None),
        P(("groups", "rows"), None, None, None),
        P(None, "rows"),
        P(None, None, "rows"),
        P(),
        P(),
        P(),
        P(None, "rows"),
    )
    return jax.shard_map(
        per_device,
        mesh=mesh,
        in_specs=placed,
        out_specs=(P(None, "groups", "rows"), P(("groups", "rows"), None, None, None)),
        check_vma=False,
    )
```

profile of v0, /device:TPU:0, one launch (start us, length us, event | category | flops | bytes accessed | tf_op | source)
XLA Modules:
  0.0 127.5 jit_solution(7853263627772895128)
XLA Ops:
  0.6 0.0 copy-start
  0.7 0.9 compare_convert_fusion.2
  1.6 0.2 reduce-window.25
  1.8 0.1 fusion.16
  2.0 2.9 %gather_fusion.3 = bf16[2,16,128,128]{3,2,1,0:T(8,128)(2,1)S(1)} fusion(bf16[8,16,128,128]{3,2,1,0:T(8,128)(2,1)} %param.13, s32[1024]{0:T(1024)S(1)} %pad_clamp_fusion.2), kind=kCustom, calls=%fused_computation.1.clone | custom fusion | bytes 2097160 | tf_op jit(solution)/shard_map/jit(_take)/gather | solution.py:35
  4.9 1.1 broadcast_select_fusion.1
  6.1 3.0 %collective-permute-start.1 = (bf16[2,16,128,128]{3,2,1,0:T(8,128)(2,1)}, bf16[2,16,128,128]{3,2,1,0:T(8,128)(2,1)}, u32[]{:S(2)}, u32[]{:S(2)}) collective-permute-start(bf16[2,16,128,128]{3,2,1,0:T(8,128)(2,1)} %broadcast_select_fusion.1), channel_id=1, source_target_pairs={{0,2},{2,0},{1,3},{3,1},{4,6},{6,4},{5,7},{7,5},{8,10},{10,8},{9,1... | collective-permute-start | bytes 3145736 | tf_op jit(solution)/shard_map/ppermute | solution.py:18
  9.1 0.2 reduce-window.24
  9.3 0.1 fusion.15
  9.4 0.0 copy-start.5
  9.4 2.9 %gather_fusion.2 = bf16[2,16,128,128]{3,2,1,0:T(8,128)(2,1)S(1)} fusion(bf16[8,16,128,128]{3,2,1,0:T(8,128)(2,1)} %param.13, s32[1024]{0:T(1024)S(1)} %pad_clamp_fusion.3), kind=kCustom, calls=%fused_computation.clone | custom fusion | bytes 2097160 | tf_op jit(solution)/shard_map/jit(_take)/gather | solution.py:35
  12.4 1.2 broadcast_select_fusion.2
  13.6 0.0 collective-permute-start
  13.6 0.2 reduce-window.26
  13.8 0.1 fusion.17
  13.9 2.9 %gather_fusion.4 = bf16[2,16,128,128]{3,2,1,0:T(8,128)(2,1)S(1)} fusion(bf16[8,16,128,128]{3,2,1,0:T(8,128)(2,1)} %param.13, s32[1024]{0:T(1024)S(1)} %pad_clamp_fusion.1), kind=kCustom, calls=%fused_computation.2.clone | custom fusion | bytes 2097160 | tf_op jit(solution)/shard_map/jit(_take)/gather | solution.py:35
  16.9 0.0 copy-start.2
  16.9 1.1 broadcast_select_fusion
  18.0 0.5 collective-permute-start.2
  18.5 0.0 copy-done.5
  18.6 5.1 %gather_fusion = bf16[128,128]{1,0:T(8,128)(2,1)S(1)} fusion(bf16[32768,128]{1,0:T(8,128)(2,1)} %param.14, s32[1024]{0:T(1024)S(1)} %pad_clamp_fusion.4), kind=kCustom, calls=%fused_computation.3 | custom fusion | bytes 66048 | tf_op jit(solution)/shard_map/jit(_take)/gather | solution.py:80
  23.7 0.1 bitcast_select_fusion
  23.8 26.1 %all_gather.6 = bf16[1,128,2048]{2,1,0:T(8,128)(2,1)S(1)} all-gather(bf16[1,128,128]{2,1,0:T(8,128)(2,1)S(1)} %bitcast_select_fusion), channel_id=1, replica_groups=mesh['groups'=2,'rows'=16] {'rows'}, dimensions={2}, use_global_device_ids=true | all-gather | bytes 557056 | tf_op jit(solution)/shard_map/all_gather | solution.py:83
  49.9 1.7 %copy.31 = bf16[2048,3,128]{0,2,1:T(8,128)(2,1)S(1)} copy(bf16[2048,3,128]{2,0,1:T(8,128)(2,1)} %param.15) | data formatting | bytes 3145728 | tf_op args[4]
  51.6 0.6 fusion.2
  52.2 0.7 copy.32
  52.9 3.5 %all-to-all-start = ((bf16[128,3,128]{2,1,0:T(4,128)(2,1)}), bf16[128,3,128]{2,1,0:T(4,128)(2,1)S(1)}, u32[]{:S(2)}, u32[]{:S(2)}) async-start(bf16[128,3,128]{2,1,0:T(4,128)(2,1)} %copy.32), calls=%async_computation | async-start | bytes 262144 | tf_op jit(solution)/shard_map/all_to_all | solution.py:90
  56.5 0.8 and_select_fusion.15
  57.2 0.2 convert_reduce_fusion
  57.5 0.0 collective-permute-done.2
  57.5 1.9 %collective-permute-start.3 = (bf16[2,16,128,128]{3,2,1,0:T(8,128)(2,1)}, bf16[2,16,128,128]{3,2,1,0:T(8,128)(2,1)S(1)}, u32[]{:S(2)}, u32[]{:S(2)}) collective-permute-start(bf16[2,16,128,128]{3,2,1,0:T(8,128)(2,1)} %collective-permute-done.2), channel_id=1, source_target_pairs={{0,2},{2,0},{1,3},{3,1},{4,6},{6,4},{5,7},{7,5},{8,10},{10,8},{9,1... | collective-permute-start | bytes 3145736 | tf_op jit(solution)/shard_map/ppermute | solution.py:18
  59.3 5.0 %all-to-all-done = bf16[128,3,128]{2,1,0:T(4,128)(2,1)S(1)} async-done(((bf16[128,3,128]{2,1,0:T(4,128)(2,1)}), bf16[128,3,128]{2,1,0:T(4,128)(2,1)S(1)}, u32[]{:S(2)}, u32[]{:S(2)}) %all-to-all-start) | async-done | bytes 98336 | tf_op jit(solution)/shard_map/all_to_all | solution.py:90
  64.4 0.1 fusion.8
  64.6 0.1 convert_multiply_fusion
  64.7 0.1 copy.34
  64.8 0.0 collective-permute-done.1
  64.8 0.0 collective-permute-done
  64.8 19.1 %collective-permute-done.3 = bf16[2,16,128,128]{3,2,1,0:T(8,128)(2,1)S(1)} collective-permute-done((bf16[2,16,128,128]{3,2,1,0:T(8,128)(2,1)}, bf16[2,16,128,128]{3,2,1,0:T(8,128)(2,1)S(1)}, u32[]{:S(2)}, u32[]{:S(2)}) %collective-permute-start.3) | collective-permute-done | bytes 1048608 | tf_op jit(solution)/shard_map/ppermute | solution.py:18
  84.0 8.1 %pad_maximum_fusion = bf16[14,16,128,128]{3,2,1,0:T(8,128)(2,1)} fusion(bf16[2,16,128,128]{3,2,1,0:T(8,128)(2,1)S(1)} %collective-permute-done.3, bf16[2,16,128,128]{3,2,1,0:T(8,128)(2,1)} %collective-permute-done.1, bf16[2,16,128,128]{3,2,1,0:T(8,128)(2,1)} %collective-permute-done, bf16[8,16,128,128]{3,2,1,0:T(8,128)(2,1)} %param.13), kind=kLoop, calls=%fused_computation.6 | loop fusion | flops 11010048 | bytes 14680064 | tf_op jit(solution)/shard_map/concatenate | solution.py:55
  92.0 6.2 %gather_fusion.1 = bf16[8,16,128,128]{3,2,1,0:T(8,128)(2,1)} fusion(bf16[14,16,128,128]{3,2,1,0:T(8,128)(2,1)} %pad_maximum_fusion, s32[1024]{0:T(1024)S(1)} %pad_clamp_fusion), kind=kCustom, calls=%fused_computation.4 | custom fusion | bytes 8388640 | tf_op jit(solution)/shard_map/jit(_take)/gather | solution.py:56
  98.2 4.6 %add_convert_fusion = bf16[8,16,128,128]{3,2,1,0:T(8,128)(2,1)S(1)} fusion(f32[8,16,128]{2,1,0:T(8,128)S(1)} %copy.36, f32[8,16,128]{2,1,0:T(8,128)S(1)} %copy.35, bf16[8,16,128,128]{3,2,1,0:T(8,128)(2,1)} %gather_fusion.1, f32[8,16]{1,0:T(8,128)S(1)} %add_divide_fusion, pred[8]{0:T(512)(128)(4,1)S(1)} %compare_and_fusion.3), kind=kLoop, calls=%fused_computation.5 | loop fusion | flops 12582912 | bytes 8520200 | tf_op jit(solution)/shard_map/convert_element_type | solution.py:103
  102.9 0.0 copy-start.1
  102.9 0.0 copy-start.3
  102.9 1.2 fusion.11
  104.1 0.1 multiply_reduce_fusion
  104.2 0.1 multiply_bitcast_fusion
  104.3 22.2 %all_gather.7 = bf16[128,2048]{1,0:T(8,128)(2,1)S(1)} all-gather(bf16[8,2048]{1,0:T(8,128)(2,1)S(1)} %fusion.10), channel_id=1, replica_groups=mesh['groups'=2,'rows'=16] {'rows'}, dimensions={0}, use_global_device_ids=true | all-gather | bytes 557056 | tf_op jit(solution)/shard_map/all_gather | solution.py:108
  126.6 0.9 fusion.6
  (37 shorter events, 0.4 us)
Async XLA Ops:
  0.6 125.9 %copy-start = (bf16[2048,128]{1,0:T(8,128)(2,1)S(1)}, bf16[2048,128]{1,0:T(8,128)(2,1)}, u32[]{:S(2)}) copy-start(bf16[2048,128]{1,0:T(8,128)(2,1)} %param.19) | copy-start | bytes 1572868
  6.1 58.7 %collective-permute-start.1 = (bf16[2,16,128,128]{3,2,1,0:T(8,128)(2,1)}, bf16[2,16,128,128]{3,2,1,0:T(8,128)(2,1)}, u32[]{:S(2)}, u32[]{:S(2)}) collective-permute-start(bf16[2,16,128,128]{3,2,1,0:T(8,128)(2,1)} %broadcast_select_fusion.1), channel_id=1, source_target_pairs={{0,2},{2,0},{1,3},{3,1},{4,6},{6,4},{5,7},{7,5},{8,10},{10,8},{9,1... | collective-permute-start | bytes 3145736 | tf_op jit(solution)/shard_map/ppermute | solution.py:18
  9.4 9.1 %copy-start.5 = (s32[1,128]{1,0:T(1,128)S(1)}, s32[1,128]{1,0:T(1,128)}, u32[]{:S(2)}) copy-start(s32[1,128]{1,0:T(1,128)} %param.11) | copy-start | bytes 1540
  13.6 51.3 %collective-permute-start = (bf16[2,16,128,128]{3,2,1,0:T(8,128)(2,1)}, bf16[2,16,128,128]{3,2,1,0:T(8,128)(2,1)}, u32[]{:S(2)}, u32[]{:S(2)}) collective-permute-start(bf16[2,16,128,128]{3,2,1,0:T(8,128)(2,1)} %broadcast_select_fusion.2), channel_id=1, source_target_pairs={{0,1},{1,0},{2,3},{3,2},{4,5},{5,4},{6,7},{7,6},{8,9},{9,8},{10,11... | collective-permute-start | bytes 3145736 | tf_op jit(solution)/shard_map/ppermute | solution.py:18
  16.9 47.6 %copy-start.2 = (f32[16,128]{1,0:T(8,128)S(1)}, f32[16,128]{1,0:T(8,128)}, u32[]{:S(2)}) copy-start(f32[16,128]{1,0:T(8,128)} %param.16) | copy-start | bytes 24580
  18.0 46.8 %copy-start.4 = (f32[16]{0:T(128)S(1)}, f32[16]{0:T(128)}, u32[]{:S(2)}) copy-start(f32[16]{0:T(128)} %param.17) | copy-start | bytes 196
  18.0 39.4 %collective-permute-start.2 = (bf16[2,16,128,128]{3,2,1,0:T(8,128)(2,1)}, bf16[2,16,128,128]{3,2,1,0:T(8,128)(2,1)}, u32[]{:S(2)}, u32[]{:S(2)}) collective-permute-start(bf16[2,16,128,128]{3,2,1,0:T(8,128)(2,1)} %broadcast_select_fusion), channel_id=1, source_target_pairs={{0,1},{1,0},{2,3},{3,2},{4,5},{5,4},{6,7},{7,6},{8,9},{9,8},{10,11... | collective-permute-start | bytes 3145736 | tf_op jit(solution)/shard_map/ppermute | solution.py:18
  52.9 11.4 %all-to-all-start = ((bf16[128,3,128]{2,1,0:T(4,128)(2,1)}), bf16[128,3,128]{2,1,0:T(4,128)(2,1)S(1)}, u32[]{:S(2)}, u32[]{:S(2)}) async-start(bf16[128,3,128]{2,1,0:T(4,128)(2,1)} %copy.32), calls=%async_computation | async-start | bytes 262144 | tf_op jit(solution)/shard_map/all_to_all | solution.py:90
  57.5 26.5 %collective-permute-start.3 = (bf16[2,16,128,128]{3,2,1,0:T(8,128)(2,1)}, bf16[2,16,128,128]{3,2,1,0:T(8,128)(2,1)S(1)}, u32[]{:S(2)}, u32[]{:S(2)}) collective-permute-start(bf16[2,16,128,128]{3,2,1,0:T(8,128)(2,1)} %collective-permute-done.2), channel_id=1, source_target_pairs={{0,2},{2,0},{1,3},{3,1},{4,6},{6,4},{5,7},{7,5},{8,10},{10,8},{9,1... | collective-permute-start | bytes 3145736 | tf_op jit(solution)/shard_map/ppermute | solution.py:18
  102.9 24.6 %copy-start.1 = (bf16[8,16,128,128]{3,2,1,0:T(8,128)(2,1)}, bf16[8,16,128,128]{3,2,1,0:T(8,128)(2,1)S(1)}, u32[]{:S(2)}) copy-start(bf16[8,16,128,128]{3,2,1,0:T(8,128)(2,1)S(1)} %add_convert_fusion) | copy-start | bytes 12582916
  102.9 1.4 %copy-start.3 = (f32[2048]{0:T(1024)S(1)}, f32[2048]{0:T(1024)}, u32[]{:S(2)}) copy-start(f32[2048]{0:T(1024)} %param.18) | copy-start | bytes 24580
where the time goes:
time: 128 us; the launch traced here: 127 us
  blocking collectives  48.4 us (38%)
  waiting for transfers between devices  24.1 us (19%)
  local copies, waits for them, and re-layouts  22.8 us (18%)
  other arithmetic  19.6 us (15%)
  starting transfers between devices  8.87 us (7%)
  matrix products  2.7 us (2%)
    all_gather x1, blocking collectives, per_device(): lax.all_gather(local_columns, 'rows', axis=2, tiled=True)  26.1 us
    all_gather x1, blocking collectives, per_device(): lax.all_gather(normed, 'rows', axis=0, tiled=True)  22.2 us
    ppermute x4, waiting for transfers between devices, from_partner(): return lax.ppermute(block, axis, route)  19.2 us
    gather x3, local copies, waits for them, and re-layouts, outgoing(): return jnp.take(state_now, chosen, axis=0)  8.82 us
    concatenate x1, other arithmetic, route(): pooled = jnp.concatenate([state_now, got_one, got_two, got_three], 0)  8.06 us
    gather x1, local copies, waits for them, and re-layouts, route(): return jnp.take(pooled, position, axis=0)  6.18 us
    ppermute x4, starting transfers between devices, from_partner(): return lax.ppermute(block, axis, route)  5.36 us
    gather x1, local copies, waits for them, and re-layouts, per_device(): local_columns = jnp.take(embed_table, token_ids, axis=0)  5.11 us
  transfers between devices with their start and end apart: 5, of which 2 were waited for; matrix products, arithmetic and copies ran while one was open for 15% of the time, Pallas kernels for 0%

commit v1 on v0

--- a/solution.py
+++ b/solution.py
@@ -1,11 +1,416 @@
+import functools
 import math
 
 import jax
 import jax.numpy as jnp
 from jax import lax
+from jax.experimental import pallas as pl
+from jax.experimental.pallas import tpu as pltpu
 from jax.sharding import PartitionSpec as P
 
 CAP = 2
+ANY = pl.BlockSpec(memory_space=pl.ANY)
+VM = pl.BlockSpec(memory_space=pltpu.VMEM)
+SM = pl.BlockSpec(memory_space=pltpu.SMEM)
+
+
+def pack_kernel(chosen_ref, state_ref, one_ref, two_ref, three_ref, buf, in_sem, out_sem):
+    outs = (one_ref, two_ref, three_ref)
+    order = [2, 3, 4, 5, 0, 1]
+    loads = {}
+    for slot in order:
+        loads[slot] = pltpu.make_async_copy(
+            state_ref.at[chosen_ref[slot]], buf.at[slot], in_sem.at[slot]
+        )
+        loads[slot].start()
+    stores = []
+    for slot in order:
+        loads[slot].wait()
+        store = pltpu.make_async_copy(
+            buf.at[slot], outs[slot // CAP].at[slot % CAP], out_sem.at[slot]
+        )
+        store.start()
+        stores.append(store)
+    for store in stores:
+        store.wait()
+
+
+def pack(chosen, states):
+    block = jax.ShapeDtypeStruct((CAP,) + states.shape[1:], states.dtype)
+    count = 3 * CAP
+    size = count * math.prod(states.shape[1:]) * 2
+    return pl.pallas_call(
+        pack_kernel,
+        out_shape=(block, block, block),
+        in_specs=[SM, ANY],
+        out_specs=(ANY, ANY, ANY),
+        scratch_shapes=[
+            pltpu.VMEM((count,) + states.shape[1:], states.dtype),
+            pltpu.SemaphoreType.DMA((count,)),
+            pltpu.SemaphoreType.DMA((count,)),
+        ],
+        cost_estimate=pl.CostEstimate(flops=0, bytes_accessed=2 * size, transcendentals=0),
+        name="pack_states",
+    )(chosen, states)
+
+
+def embed_kernel(tok_ref, table_ref, out_ref, buf, wide, rows_out, sem):
+    count = out_ref.shape[0]
+
+    def begin(i, _):
+        pltpu.make_async_copy(table_ref.at[tok_ref[i] // 8], buf.at[i], sem).start()
+        return _
+
+    lax.fori_loop(0, count, begin, 0, unroll=8)
+    pltpu.make_async_copy(table_ref.at[pl.ds(0, count)], buf, sem).wait()
+    wide[...] = buf[...].astype(jnp.float32).reshape(wide.shape)
+
+    def pick(i, _):
+        rows_out[pl.ds(i, 1), :] = wide[pl.ds(i * 8 + tok_ref[i] % 8, 1), :]
+        return _
+
+    lax.fori_loop(0, count, pick, 0, unroll=8)
+    out_ref[...] = rows_out[...].astype(jnp.bfloat16)
+
+
+def embed(tokens, table):
+    count, width = tokens.shape[0], table.shape[1]
+    return pl.pallas_call(
+        embed_kernel,
+        out_shape=jax.ShapeDtypeStruct((count, width), table.dtype),
+        in_specs=[SM, ANY],
+        out_specs=VM,
+        scratch_shapes=[
+            pltpu.VMEM((count, 8, width), table.dtype),
+            pltpu.VMEM((count * 8, width), jnp.float32),
+            pltpu.VMEM((count, width), jnp.float32),
+            pltpu.SemaphoreType.DMA,
+        ],
+        cost_estimate=pl.CostEstimate(
+            flops=0, bytes_accessed=count * 8 * width * 2, transcendentals=0
+        ),
+        name="embed_rows",
+    )(tokens, table.reshape(table.shape[0] // 8, 8, width))
+
+
+def greet(peers):
+    barrier = pltpu.get_barrier_semaphore()
+    for peer in peers:
+        pl.semaphore_signal(
+            barrier, inc=1, device_id={"rows": peer}, device_id_type=pl.DeviceIdType.MESH
+        )
+    pl.semaphore_wait(barrier, len(peers))
+
+
+def spread_kernel(count, spans, mode, in_ref, out_ref, send_sem, recv_sem, own_sem):
+    me = lax.axis_index("rows")
+    level = count // 4
+    member = me % 4
+    my_level = me // 4
+    side = my_level * 4 + (member + 2) % 4
+    twin = my_level * 4 + member + 1 - 2 * (member % 2)
+    side_twin = my_level * 4 + (twin % 4 + 2) % 4
+    peers = [((my_level + k) % level) * 4 + member for k in range(1, level)]
+    side_peers = [((my_level + k) % level) * 4 + (member + 2) % 4 for k in range(1, level)]
+
+    def place(block):
+        if mode == "columns":
+            return out_ref.at[:, pl.ds(pl.multiple_of(block * spans, spans), spans)]
+        return out_ref.at[pl.ds(pl.multiple_of(block * spans, spans), spans)]
+
+    sent = []
+
+    def send(source, block, target):
+        copy = pltpu.make_async_remote_copy(
+            src_ref=source,
+            dst_ref=place(block),
+            send_sem=send_sem.at[len(sent)],
+            recv_sem=recv_sem.at[block],
+            device_id={"rows": target},
+            device_id_type=pl.DeviceIdType.MESH,
+        )
+        copy.start()
+        sent.append(copy)
+
+    def arrived(block):
+        pltpu.make_async_remote_copy(
+            src_ref=place(block),
+            dst_ref=place(block),
+            send_sem=send_sem.at[0],
+            recv_sem=recv_sem.at[block],
+            device_id={"rows": twin},
+            device_id_type=pl.DeviceIdType.MESH,
+        ).wait_recv()
+
+    greet([side, twin] + peers)
+    if mode == "exchange":
+        def part(owner):
+            return in_ref.at[pl.ds(pl.multiple_of(owner * spans, spans), spans)]
+
+        for peer in reversed(peers):
+            send(part(peer // 4), me, peer)
+        mine = part(my_level)
+        send(mine, me, side)
+        send(mine, me, twin)
+        own = pltpu.make_async_copy(mine, place(me), own_sem)
+        own.start()
+        for peer in peers:
+            arrived(peer)
+            send(place(peer), peer, side)
+            send(place(peer), peer, twin)
+        arrived(side)
+        send(place(side), side, twin)
+        for peer in side_peers:
+            arrived(peer)
+            send(place(peer), peer, twin)
+    else:
+        send(in_ref, me, side)
+        for peer in peers:
+            send(in_ref, me, peer)
+        send(in_ref, me, twin)
+        own = pltpu.make_async_copy(in_ref, place(me), own_sem)
+        own.start()
+        arrived(side)
+        for peer in peers:
+            send(place(side), side, peer)
+        send(place(side), side, twin)
+        for k in range(level - 1):
+            arrived(peers[k])
+            send(place(peers[k]), peers[k], twin)
+        for k in range(level - 1):
+            arrived(side_peers[k])
+            send(place(side_peers[k]), side_peers[k], twin)
+    arrived(twin)
+    arrived(side_twin)
+    for k in range(1, level):
+        base = ((my_level + k) % level) * 4
+        arrived(base + twin % 4)
+        arrived(base + side_twin % 4)
+    own.wait()
+    for copy in sent:
+        copy.wait_send()
+
+
+def spread(block, count, spans, mode, out_shape, identity, name):
+    return pl.pallas_call(
+        functools.partial(spread_kernel, count, spans, mode),
+        out_shape=jax.ShapeDtypeStruct(out_shape, block.dtype),
+        in_specs=[VM],
+        out_specs=VM,
+        scratch_shapes=[
+            pltpu.SemaphoreType.DMA((count - 1,)),
+            pltpu.SemaphoreType.DMA((count,)),
+            pltpu.SemaphoreType.DMA,
+        ],
+        compiler_params=pltpu.CompilerParams(collective_id=identity, has_side_effects=True),
+        cost_estimate=pl.CostEstimate(
+            flops=0, bytes_accessed=16 * math.prod(out_shape), transcendentals=0
+        ),
+        name=name,
+    )(block)
+
+
+def read_kernel(
+    head_size, bias_ref, qkv_ref, state_ref, weight_ref, gain_ref, owner_ref, slot_ref, out_ref
+):
+    head = pl.program_id(0)
+    block = qkv_ref[0]
+    queries = block[:, :head_size].astype(jnp.float32)
+    keys = block[:, head_size : 2 * head_size].astype(jnp.float32)
+    values = block[:, 2 * head_size :].astype(jnp.float32)
+    logit = jnp.sum(keys * weight_ref[0], axis=-1, keepdims=True) / math.sqrt(head_size)
+    decay = jax.nn.sigmoid(logit + bias_ref[head])
+    unit = keys * lax.rsqrt(jnp.sum(keys * keys, axis=-1, keepdims=True) + 1e-06)
+    total = jnp.zeros(queries.shape, jnp.float32)
+    for parent in range(state_ref.shape[0]):
+        chosen = (queries * owner_ref[:, parent : parent + 1]).astype(jnp.bfloat16)
+        total += jnp.dot(chosen, state_ref[parent, 0], preferred_element_type=jnp.float32)
+    readout = decay * total + jnp.sum(queries * unit, axis=-1, keepdims=True) * values
+    scaled = readout * lax.rsqrt(jnp.mean(readout * readout, axis=-1, keepdims=True) + 1e-05)
+    normed = (scaled * gain_ref[0]).astype(jnp.bfloat16)
+    out_ref[...] = jnp.dot(slot_ref[...], normed, preferred_element_type=jnp.float32).astype(
+        jnp.bfloat16
+    )
+
+
+def read(qkv, states, gate_weight, gate_bias, norm_gain, owner, slot_pick):
+    heads, beams, triple = qkv.shape
+    row_local, _, head_size, _ = states.shape
+    slots = slot_pick.shape[0]
+    return pl.pallas_call(
+        functools.partial(read_kernel, head_size),
+        grid=(heads,),
+        out_shape=jax.ShapeDtypeStruct((slots, heads * head_size), jnp.bfloat16),
+        in_specs=[
+            SM,
+            pl.BlockSpec((1, beams, triple), lambda h: (h, 0, 0)),
+            pl.BlockSpec((row_local, 1, head_size, head_size), lambda h: (0, h, 0, 0)),
+            pl.BlockSpec((1, 1, head_size), lambda h: (h, 0, 0)),
+            pl.BlockSpec((1, 1, head_size), lambda h: (h, 0, 0)),
+            pl.BlockSpec((beams, row_local), lambda h: (0, 0)),
+            pl.BlockSpec((slots, beams), lambda h: (0, 0)),
+        ],
+        out_specs=pl.BlockSpec((slots, head_size), lambda h: (0, h)),
+        cost_estimate=pl.CostEstimate(
+            flops=2 * beams * math.prod(states.shape),
+            bytes_accessed=2 * math.prod(states.shape),
+            transcendentals=0,
+        ),
+        name="read_heads",
+    )(
+        gate_bias,
+        qkv,
+        states,
+        gate_weight.reshape(heads, 1, head_size),
+        norm_gain.reshape(heads, 1, head_size),
+        owner,
+        slot_pick,
+    )
+
+
+def update_kernel(
+    kind_ref, index_ref, decay_ref, state_ref, one_ref, two_ref, three_ref, unit_ref, value_ref,
+    out_ref, old, new, in_sem, out_sem
+):
+    row_local, heads = old.shape[0], old.shape[1]
+    sources = (state_ref, one_ref, two_ref, three_ref)
+    for row in range(row_local):
+        for kind, source in enumerate(sources):
+            @pl.when(kind_ref[row] == kind)
+            def _():
+                pltpu.make_async_copy(
+                    source.at[index_ref[row]], old.at[row], in_sem.at[row]
+                ).start()
+
+    def step(row, carry):
+        pltpu.make_async_copy(state_ref.at[0], old.at[row], in_sem.at[row]).wait()
+        columns = unit_ref[row]
+        values = value_ref[row]
+        for head in range(heads):
+            fresh = columns[:, head : head + 1] * values[head : head + 1, :]
+            prior = old[row, head].astype(jnp.float32)
+            new[row, head] = (decay_ref[row, head] * prior + fresh).astype(jnp.bfloat16)
+        pltpu.make_async_copy(new.at[row], out_ref.at[row], out_sem.at[row]).start()
+        return carry
+
+    lax.fori_loop(0, row_local, step, 0)
+    for row in range(row_local):
+        pltpu.make_async_copy(new.at[row], out_ref.at[row], out_sem.at[row]).wait()
+
+
+def update(kind, index, decay, states, one, two, three, unit, values):
+    row_local = states.shape[0]
+    return pl.pallas_call(
+        update_kernel,
+        out_shape=jax.ShapeDtypeStruct(states.shape, states.dtype),
+        in_specs=[SM, SM, SM, ANY, ANY, ANY, ANY, VM, VM],
+        out_specs=ANY,
+        scratch_shapes=[
+            pltpu.VMEM(states.shape, states.dtype),
+            pltpu.VMEM(states.shape, states.dtype),
+            pltpu.SemaphoreType.DMA((row_local,)),
+            pltpu.SemaphoreType.DMA((row_local,)),
+        ],
+        cost_estimate=pl.CostEstimate(
+            flops=4 * math.prod(states.shape),
+            bytes_accessed=4 * math.prod(states.shape),
+            transcendentals=0,
+        ),
+        name="update_states",
+    )(kind, index, decay, states, one, two, three, unit, values)
+
+
+def swap(block, partner):
+    count = lax.axis_size("rows")
+    return lax.ppermute(block, "rows", [(low, low ^ partner) for low in range(count)])
+
+
+def fast(
+    token_ids, parents, states, embed_table, qkv_weight, gate_weight, gate_bias, norm_gain,
+    out_weight
+):
+    row_local, heads, head_size, _ = states.shape
+    width = heads * head_size
+    column_local = embed_table.shape[1]
+    row_total = token_ids.shape[1]
+    users, beams = parents.shape[1], parents.shape[2]
+    count = lax.axis_size("rows")
+    device = lax.axis_index("rows")
+    member, user = device % 4, device // 4
+    slots = 16 * ((row_local + 3 * CAP + 15) // 16)
+
+    lists = parents[0]
+    owner_block = lists // row_local
+    blocks = owner_block.reshape(users, 4, row_local)
+    at = jnp.arange(row_local, dtype=jnp.int32)
+    same = (blocks[..., :, None] == blocks[..., None, :]) & (at[:, None] > at[None, :])
+    rank = jnp.sum(same.astype(jnp.int32), axis=-1)
+    offset = jnp.bitwise_xor(blocks, jnp.arange(4, dtype=jnp.int32)[None, :, None])
+    slot = jnp.where(offset == 0, at[None, None, :], row_local + (offset - 1) * CAP + rank)
+    slot = slot.reshape(users, beams)
+    my_list = lax.dynamic_index_in_dim(lists, user, 0, keepdims=False)
+    my_slot = lax.dynamic_index_in_dim(slot, user, 0, keepdims=False)
+    held = my_list // row_local == member
+    within = my_list % row_local
+    slot_pick = held[None, :] & (my_slot[None, :] == jnp.arange(slots, dtype=jnp.int32)[:, None])
+    chosen = jnp.sum(
+        jnp.where(slot_pick[row_local : row_local + 3 * CAP], within[None, :], 0), axis=1
+    )
+    owner = (held[:, None] & (within[:, None] == at[None, :])).astype(jnp.float32)
+    own_slot = lax.dynamic_slice_in_dim(my_slot, member * row_local, row_local, 0)
+    own_within = lax.dynamic_slice_in_dim(within, member * row_local, row_local, 0)
+    far = own_slot >= row_local
+    kind = jnp.where(far, (own_slot - row_local) // CAP + 1, 0)
+    index = jnp.where(far, (own_slot - row_local) % CAP, own_within)
+
+    one, two, three = pack(chosen, states)
+    got_two = swap(two, 2)
+    got_three = swap(three, 3)
+    got_one = swap(one, 1)
+
+    local_columns = embed(token_ids[0], embed_table)
+    every_input = spread(
+        local_columns, count, column_local, "columns", (row_total, count * column_local), 1,
+        "spread_inputs"
+    )
+    projected = jnp.dot(
+        every_input,
+        qkv_weight.reshape(qkv_weight.shape[0], 3 * column_local),
+        preferred_element_type=jnp.float32,
+    ).astype(jnp.bfloat16)
+    qkv = spread(
+        projected.reshape(row_total, 3 * column_local), count, beams, "exchange",
+        (count * beams, 3 * column_local), 2, "spread_heads"
+    ).reshape(count, beams, 3 * column_local)
+    normed = read(
+        qkv, states, gate_weight, gate_bias, norm_gain, owner, slot_pick.astype(jnp.bfloat16)
+    )
+    every_normed = spread(
+        normed, count, slots, "rows", (count * slots, width), 3, "spread_normed"
+    )
+    source = (
+        (jnp.arange(users, dtype=jnp.int32)[:, None] * 4 + owner_block) * slots + slot
+    ).reshape(row_total)
+    pick = (source[:, None] == jnp.arange(count * slots, dtype=jnp.int32)[None, :]).astype(
+        jnp.bfloat16
+    )
+    ordered = jnp.dot(pick, every_normed, preferred_element_type=jnp.float32)
+    attention = jnp.dot(
+        ordered.astype(jnp.bfloat16), out_weight, preferred_element_type=jnp.float32
+    )
+    layer_out = (local_columns.astype(jnp.float32) + attention).astype(jnp.bfloat16)
+
+    mine = lax.dynamic_slice_in_dim(qkv, member * row_local, row_local, 1)
+    keys = mine[:, :, head_size : 2 * head_size].astype(jnp.float32)
+    values = jnp.swapaxes(mine[:, :, 2 * head_size :].astype(jnp.float32), 0, 1)
+    logit = jnp.sum(keys * gate_weight[:, None, :], axis=-1) / math.sqrt(head_size)
+    decay = jax.nn.sigmoid(logit + gate_bias[:, None]).T
+    unit = keys * lax.rsqrt(jnp.sum(keys * keys, axis=-1, keepdims=True) + 1e-06)
+    state_now = update(
+        kind, index, decay, states, got_one, got_two, got_three, jnp.transpose(unit, (1, 2, 0)),
+        values
+    )
+    return (layer_out[None], state_now)
 
 
 def from_partner(block, axis, stride):
@@ -70,6 +475,20 @@
     row_local = states.shape[0]
     heads = states.shape[1]
     head_size = states.shape[2]
+    count = lax.axis_size("rows")
+    if (
+        embed_table.shape[1] == head_size
+        and head_size % 128 == 0
+        and count == heads
+        and parents.shape[0] == 1
+        and parents.shape[2] == 4 * row_local
+        and parents.shape[1] * 4 == count
+        and parents.shape[2] % 16 == 0
+    ):
+        return fast(
+            token_ids, parents, states, embed_table, qkv_weight, gate_weight, gate_bias,
+            norm_gain, out_weight
+        )
     width = heads * head_size
     column_local = embed_table.shape[1]
     row_total = token_ids.shape[1]

time: 128 us -> 126 us (0.984)
  Pallas kernels: 0 us -> 107 us
  blocking collectives: 48.4 us -> 0 us
  waiting for transfers between devices: 24.1 us -> 0.01 us
  local copies, waits for them, and re-layouts: 22.8 us -> 5.2 us
  other arithmetic: 19.6 us -> 5.79 us
  starting transfers between devices: 8.87 us -> 3.34 us
    pallas_call x0 -> x7, Pallas kernels: none -> 107 us  [the longest x3 80.3 us: spread(): pl.pallas_call(functools.partial(spread_kernel, count, spans, mode), out_...]
    all_gather x2 -> x0, blocking collectives: 48.4 us -> none  [the longest x1 26.1 us: per_device(): lax.all_gather(local_columns, 'rows', axis=2, tiled=True)]
    gather x5 -> x0, local copies, waits for them, and re-layouts: 20.1 us -> none  [the longest x3 8.82 us: outgoing(): return jnp.take(state_now, chosen, axis=0)]
    ppermute x4 -> x3, waiting for transfers between devices: 19.2 us -> 0.01 us  [swap(): lax.ppermute(block, 'rows', [(low, low ^ partner) for low in range(count)])]
    concatenate x1 -> x0, other arithmetic: 8.06 us -> none  [route(): pooled = jnp.concatenate([state_now, got_one, got_two, got_three], 0)]
    all_to_all x1 -> x0, waiting for transfers between devices: 4.99 us -> none  [per_device(): lax.all_to_all(projected, 'rows', split_axis=0, concat_axis=2, tiled=True)]
    convert_element_type x3 -> x1, other arithmetic: 5.55 us -> 0.68 us  [fast(): (held[:, None] & (within[:, None] == at[None, :])).astype(jnp.float32)]
    all_to_all x1 -> x0, starting transfers between devices: 3.51 us -> none  [per_device(): lax.all_to_all(projected, 'rows', split_axis=0, concat_axis=2, tiled=True)]
  transfers between devices with their start and end apart: 5 -> 3, of which waited for: 2 -> 0; matrix products, arithmetic and copies ran while one was open for 15% -> 8% of each run, Pallas kernels for 0% -> 77%
where the time goes in v1:
time: 126 us
  Pallas kernels  107 us (85%)
  other arithmetic  5.79 us (5%)
  local copies, waits for them, and re-layouts  5.2 us (4%)
  matrix products  3.56 us (3%)
  starting transfers between devices  3.34 us (3%)
    pallas_call x3, Pallas kernels, spread(): pl.pallas_call(functools.partial(spread_kernel, count, spans, mode), out_...  80.3 us
    pallas_call x1, Pallas kernels, read(): pl.pallas_call(functools.partial(read_kernel, head_size), grid=(heads,),...  12.8 us
    pallas_call x1, Pallas kernels, update(): pl.pallas_call(update_kernel, out_shape=jax.ShapeDtypeStruct(states.shape...  5.96 us
    pallas_call x1, Pallas kernels, pack(): pl.pallas_call(pack_kernel, out_shape=(block, block, block), in_specs=[SM...  4.4 us
    pallas_call x1, Pallas kernels, embed(): pl.pallas_call(embed_kernel, out_shape=jax.ShapeDtypeStruct((count, width...  3.5 us
    ppermute x3, starting transfers between devices, swap(): lax.ppermute(block, 'rows', [(low, low ^ partner) for low in range(count)])  3.34 us
  transfers between devices with their start and end apart: 3, of which 0 were waited for; matrix products, arithmetic and copies ran while one was open for 8% of the time, Pallas kernels for 77%

profile of v1, /device:TPU:0, one launch (start us, length us, event | category | flops | bytes accessed | tf_op | source)
XLA Modules:
  0.0 125.7 jit_solution(795736618749557671)
XLA Ops:
  0.6 0.0 copy-start
  0.7 0.8 squeeze.17
  1.5 0.7 fusion.21
  2.2 0.1 broadcast_in_dim.55
  2.3 0.1 xor.28
  2.4 0.4 convert_reduce_fusion
  2.8 0.1 reduce_sum.42
  2.9 0.7 add_select_fusion.2
  3.6 0.6 fusion.13
  4.2 0.6 select_reduce_fusion.chosen_ref
  4.9 4.4 %pack_states.1 = (bf16[2,16,128,128]{3,2,1,0:T(8,128)(2,1)}, bf16[2,16,128,128]{3,2,1,0:T(8,128)(2,1)}, bf16[2,16,128,128]{3,2,1,0:T(8,128)(2,1)}) custom-call(s32[6]{0:T(128)} %select_reduce_fusion.chosen_ref, bf16[8,16,128,128]{3,2,1,0:T(8,128)(2,1)} %state_ref.5), custom_call_target="tpu_custom_call" | custom-call | bytes 6291456 | tf_op jit(solution)/shard_map/pack_states/pallas_call | solution.py:42
  9.3 0.6 collective-permute-start
  9.9 2.7 %collective-permute-start.1 = (bf16[2,16,128,128]{3,2,1,0:T(8,128)(2,1)}, bf16[2,16,128,128]{3,2,1,0:T(8,128)(2,1)}, u32[]{:S(2)}, u32[]{:S(2)}) collective-permute-start(bf16[2,16,128,128]{3,2,1,0:T(8,128)(2,1)} %get-tuple-element.6), channel_id=1, source_target_pairs={{0,2},{1,3},{2,0},{3,1},{4,6},{5,7},{6,4},{7,5},{8,10},{9,11},{10,... | collective-permute-start | bytes 3145736 | tf_op jit(solution)/shard_map/ppermute | solution.py:325
  12.6 0.0 collective-permute-start.2
  12.6 0.0 copy-done.4
  12.6 0.1 squeeze.16
  12.7 0.1 reduce_sum.41
  12.8 0.7 fusion.10.owner_ref
  13.5 3.5 %embed_rows.1.in_ref = bf16[128,128]{1,0:T(8,128)(2,1)} custom-call(s32[128]{0:T(128)} %bitcast.71, bf16[4096,8,128]{2,1,0:T(8,128)(2,1)} %bitcast.65), custom_call_target="tpu_custom_call" | custom-call | bytes 262144 | tf_op jit(solution)/shard_map/embed_rows/pallas_call | solution.py:78
  17.0 50.2 %spread_inputs.1 = bf16[128,2048]{1,0:T(8,128)(2,1)} custom-call(bf16[128,128]{1,0:T(8,128)(2,1)} %embed_rows.1.in_ref), custom_call_target="tpu_custom_call" | custom-call | bytes 4194304 | tf_op jit(solution)/shard_map/spread_inputs/pallas_call | solution.py:195
  67.2 0.0 copy-start.1
  67.2 1.8 %copy.16 = bf16[2048,3,128]{0,2,1:T(8,128)(2,1)S(1)} copy(bf16[2048,3,128]{2,0,1:T(8,128)(2,1)} %param.13) | data formatting | bytes 3145728 | tf_op args[4]
  69.0 0.0 copy-start.3
  69.0 0.0 copy-done.1
  69.0 1.2 convolution_convert_fusion.1.in_ref
  70.2 12.7 %spread_heads.1 = bf16[512,384]{1,0:T(8,128)(2,1)} custom-call(bf16[128,384]{1,0:T(8,128)(2,1)} %convolution_convert_fusion.1.in_ref), custom_call_target="tpu_custom_call" | custom-call | bytes 3145728 | tf_op jit(solution)/shard_map/spread_heads/pallas_call | solution.py:195
  82.9 0.8 constant_dynamic-slice_fusion.1
  83.7 0.0 copy-done.3
  83.7 0.1 fusion.5
  83.8 0.1 fusion.6
  83.9 0.1 add.148
  84.0 0.1 add.149
  84.1 0.1 broadcast_in_dim.57
  84.2 0.1 xor.30
  84.3 1.0 copy.18.unit_ref
  85.3 12.8 %read_heads.1.in_ref = bf16[16,2048]{1,0:T(8,128)(2,1)} custom-call(f32[16]{0:T(128)} %bias_ref.1, bf16[16,32,384]{2,1,0:T(8,128)(2,1)} %bitcast.68, bf16[8,16,128,128]{3,2,1,0:T(8,128)(2,1)} %state_ref.5, f32[16,1,128]{2,1,0:T(1,128)} %bitcast.69, f32[16,1,128]{2,1,0:T(1,128)} %bitcast.70, f32[32,8]{1,0:T(8,128)} %fusion.10.owner_ref, ...), custom_call_target="tpu_custom_call" | custom-call | flops 134217728 | bytes 4194304 | tf_op jit(solution)/shard_map/read_heads/pallas_call | solution.py:240
  98.1 17.4 %spread_normed.1 = bf16[256,2048]{1,0:T(8,128)(2,1)} custom-call(bf16[16,2048]{1,0:T(8,128)(2,1)} %read_heads.1.in_ref), custom_call_target="tpu_custom_call" | custom-call | bytes 8388608 | tf_op jit(solution)/shard_map/spread_normed/pallas_call | solution.py:195
  115.5 0.6 bitcast_select_fusion
  116.1 0.0 copy-done
  116.2 0.0 copy-done.2
  116.2 2.3 %fusion.3 = bf16[1,128,128]{2,1,0:T(8,128)(2,1)} fusion(bf16[2048,128]{1,0:T(8,128)(2,1)S(1)} %copy-done, bf16[256,2048]{1,0:T(8,128)(2,1)} %spread_normed.1, s32[128]{0:T(128)S(1)} %fusion.20, bf16[128,128]{1,0:T(8,128)(2,1)S(1)} %copy-done.2), kind=kOutput, calls=%fused_computation.5 | convolution fusion | flops 201670656 | bytes 1638912 | tf_op jit(solution)/shard_map/dot_general | solution.py:398
  118.5 0.0 copy-done.5
  118.5 0.6 divide_bitcast_fusion.decay_ref
  119.1 0.6 convert_bitcast_fusion.value_ref
  119.7 0.0 collective-permute-done.one_ref
  119.7 0.0 collective-permute-done.1.two_ref
  119.7 0.0 collective-permute-done.2.three_ref
  119.7 6.0 %update_states.1 = bf16[8,16,128,128]{3,2,1,0:T(8,128)(2,1)} custom-call(s32[8]{0:T(128)} %get-tuple-element.15.kind_ref, s32[8]{0:T(128)} %get-tuple-element.14.index_ref, f32[8,16]{1,0:T(8,128)} %divide_bitcast_fusion.decay_ref, bf16[8,16,128,128]{3,2,1,0:T(8,128)(2,1)} %state_ref.5, bf16[2,16,128,128]{3,2,1,0:T(8,128)(2,1)} %collective-permute-done.one_ref, ...), custom_call_target="tpu_custom_call" | custom-call | flops 8388608 | bytes 8388608 | tf_op jit(solution)/shard_map/update_states/pallas_call | solution.py:303
  (14 shorter events, 0.1 us)
Async XLA Ops:
  0.6 115.5 %copy-start = (bf16[2048,128]{1,0:T(8,128)(2,1)S(1)}, bf16[2048,128]{1,0:T(8,128)(2,1)}, u32[]{:S(2)}) copy-start(bf16[2048,128]{1,0:T(8,128)(2,1)} %param.17) | copy-start | bytes 1572868
  4.9 7.8 %copy-start.4 = (s32[1,4,32]{2,1,0:T(4,128)S(1)}, s32[1,4,32]{2,1,0:T(4,128)}, u32[]{:S(2)}) copy-start(s32[1,4,32]{2,1,0:T(4,128)} %param.10) | copy-start | bytes 1540
  9.3 110.4 %collective-permute-start = (bf16[2,16,128,128]{3,2,1,0:T(8,128)(2,1)}, bf16[2,16,128,128]{3,2,1,0:T(8,128)(2,1)}, u32[]{:S(2)}, u32[]{:S(2)}) collective-permute-start(bf16[2,16,128,128]{3,2,1,0:T(8,128)(2,1)} %get-tuple-element.5), channel_id=1, source_target_pairs={{0,1},{1,0},{2,3},{3,2},{4,5},{5,4},{6,7},{7,6},{8,9},{9,8},{10,11... | collective-permute-start | bytes 3145736 | tf_op jit(solution)/shard_map/ppermute | solution.py:325
  9.9 109.8 %collective-permute-start.1 = (bf16[2,16,128,128]{3,2,1,0:T(8,128)(2,1)}, bf16[2,16,128,128]{3,2,1,0:T(8,128)(2,1)}, u32[]{:S(2)}, u32[]{:S(2)}) collective-permute-start(bf16[2,16,128,128]{3,2,1,0:T(8,128)(2,1)} %get-tuple-element.6), channel_id=1, source_target_pairs={{0,2},{1,3},{2,0},{3,1},{4,6},{5,7},{6,4},{7,5},{8,10},{9,11},{10,... | collective-permute-start | bytes 3145736 | tf_op jit(solution)/shard_map/ppermute | solution.py:325
  12.6 107.1 %collective-permute-start.2 = (bf16[2,16,128,128]{3,2,1,0:T(8,128)(2,1)}, bf16[2,16,128,128]{3,2,1,0:T(8,128)(2,1)}, u32[]{:S(2)}, u32[]{:S(2)}) collective-permute-start(bf16[2,16,128,128]{3,2,1,0:T(8,128)(2,1)} %get-tuple-element.7), channel_id=1, source_target_pairs={{0,3},{1,2},{2,1},{3,0},{4,7},{5,6},{6,5},{7,4},{8,11},{9,10},{10,... | collective-permute-start | bytes 3145736 | tf_op jit(solution)/shard_map/ppermute | solution.py:325
  67.2 1.8 %copy-start.1 = (bf16[128,2048]{1,0:T(8,128)(2,1)S(1)}, bf16[128,2048]{1,0:T(8,128)(2,1)}, u32[]{:S(2)}) copy-start(bf16[128,2048]{1,0:T(8,128)(2,1)} %spread_inputs.1) | copy-start | bytes 1572868
  69.0 14.7 %copy-start.3 = (f32[16,128]{1,0:T(8,128)S(1)}, f32[16,128]{1,0:T(8,128)}, u32[]{:S(2)}) copy-start(f32[16,128]{1,0:T(8,128)} %param.14) | copy-start | bytes 24580
  85.3 30.9 %copy-start.2 = (bf16[128,128]{1,0:T(8,128)(2,1)S(1)}, bf16[128,128]{1,0:T(8,128)(2,1)}, u32[]{:S(2)}) copy-start(bf16[128,128]{1,0:T(8,128)(2,1)} %embed_rows.1.in_ref) | copy-start | bytes 98308
  98.1 20.4 %copy-start.5 = (f32[16]{0:T(128)S(1)}, f32[16]{0:T(128)}, u32[]{:S(2)}) copy-start(f32[16]{0:T(128)} %bias_ref.1) | copy-start | bytes 196

commit v2 on v1

v2 whole, which is shorter than its diff:
```python
import functools
import math

import jax
import jax.numpy as jnp
from jax import lax
from jax.experimental import pallas as pl
from jax.experimental.pallas import tpu as pltpu
from jax.sharding import PartitionSpec as P

CAP = 2
ANY = pl.BlockSpec(memory_space=pl.ANY)
VM = pl.BlockSpec(memory_space=pltpu.VMEM)
SM = pl.BlockSpec(memory_space=pltpu.SMEM)


def gather_kernel(
    level, list_ref, tok_ref, state_ref, table_ref, one_ref, far_ref, out_ref,
    buf, rows_in, wide, rows_out, in_sem, out_sem, row_sem
):
    device = lax.axis_index("rows")
    member, user = device % 4, device // 4
    row_local = state_ref.shape[0]
    loads = []
    for slot in list(range(CAP, 3 * CAP)) + list(range(CAP)):
        partner, order = slot // CAP + 1, slot % CAP
        base = jnp.bitwise_xor(member, partner) * row_local
        seen, chosen = jnp.int32(0), jnp.int32(0)
        for child in range(row_local):
            parent = list_ref[0, user, base + child]
            needed = parent // row_local == member
            chosen = jnp.where(needed & (seen == order), parent % row_local, chosen)
            seen = seen + needed.astype(jnp.int32)
        load = pltpu.make_async_copy(state_ref.at[chosen], buf.at[slot], in_sem.at[slot])
        load.start()
        loads.append((slot, load))
    count = out_ref.shape[0]

    def begin(i, carry):
        pltpu.make_async_copy(table_ref.at[tok_ref[0, i] // 8], rows_in.at[i], row_sem).start()
        return carry

    lax.fori_loop(0, count, begin, 0, unroll=8)
    stores = []
    for slot, load in loads:
        load.wait()
        target = one_ref.at[slot] if slot < CAP else far_ref.at[slot - CAP]
        store = pltpu.make_async_copy(buf.at[slot], target, out_sem.at[slot])
        store.start()
        stores.append(store)
    pltpu.make_async_copy(table_ref.at[pl.ds(0, count)], rows_in, row_sem).wait()
    wide[...] = rows_in[...].astype(jnp.float32).reshape(wide.shape)

    def pick(i, carry):
        rows_out[pl.ds(i, 1), :] = wide[pl.ds(i * 8 + tok_ref[0, i] % 8, 1), :]
        return carry

    lax.fori_loop(0, count, pick, 0, unroll=8)
    out_ref[...] = rows_out[...].astype(jnp.bfloat16)
    for store in stores:
        store.wait()


def gather(parents, tokens, states, table):
    rest = states.shape[1:]
    slots = 3 * CAP
    count, width = tokens.shape[1], table.shape[1]
    size = slots * math.prod(rest) * 2
    return pl.pallas_call(
        functools.partial(gather_kernel, parents.shape[1]),
        out_shape=(
            jax.ShapeDtypeStruct((CAP,) + rest, states.dtype),
            jax.ShapeDtypeStruct((2 * CAP,) + rest, states.dtype),
            jax.ShapeDtypeStruct((count, width), table.dtype),
        ),
        in_specs=[SM, SM, ANY, ANY],
        out_specs=(ANY, ANY, VM),
        scratch_shapes=[
            pltpu.VMEM((slots,) + rest, states.dtype),
            pltpu.VMEM((count, 8, width), table.dtype),
            pltpu.VMEM((count * 8, width), jnp.float32),
            pltpu.VMEM((count, width), jnp.float32),
            pltpu.SemaphoreType.DMA((slots,)),
            pltpu.SemaphoreType.DMA((slots,)),
            pltpu.SemaphoreType.DMA,
        ],
        cost_estimate=pl.CostEstimate(flops=0, bytes_accessed=2 * size, transcendentals=0),
        name="gather_rows",
    )(parents, tokens, states, table.reshape(table.shape[0] // 8, 8, width))


def greet(peers):
    barrier = pltpu.get_barrier_semaphore()
    for peer in peers:
        pl.semaphore_signal(
            barrier, inc=1, device_id={"rows": peer}, device_id_type=pl.DeviceIdType.MESH
        )
    pl.semaphore_wait(barrier, len(peers))


def spread_kernel(count, spans, mode, first, heads, near, *refs):
    refs = list(refs)
    in_ref, far_ref = refs[0], refs[1]
    one_ref = refs.pop(2) if near else None
    out_ref, got_ref = refs[2], refs[3]
    got_one_ref = refs.pop(4) if near else None
    stage, send_sem, recv_sem, own_sem, bulk_send, bulk_recv = refs[4:]
    me = lax.axis_index("rows")
    level = count // 4
    member = me % 4
    my_level = me // 4
    side_member = (member + 2) % 4
    twin_member = member + 1 - 2 * (member % 2)
    diag_member = (twin_member + 2) % 4
    side = my_level * 4 + side_member
    twin = my_level * 4 + twin_member
    diag = my_level * 4 + diag_member
    levels = [(my_level + k) % level for k in range(1, level)]
    peers = [other * 4 + member for other in levels]
    side_peers = [other * 4 + side_member for other in levels]

    def place(block):
        if mode == "columns":
            return out_ref.at[:, pl.ds(pl.multiple_of(block * spans, spans), spans)]
        return out_ref.at[pl.ds(pl.multiple_of(block * spans, spans), spans)]

    def part(ref, other):
        if mode == "exchange":
            return ref.at[pl.ds(pl.multiple_of(other * spans, spans), spans)]
        return ref

    def remote(source, target_ref, out_sem, in_sem, target):
        return pltpu.make_async_remote_copy(
            src_ref=source,
            dst_ref=target_ref,
            send_sem=out_sem,
            recv_sem=in_sem,
            device_id={"rows": target},
            device_id_type=pl.DeviceIdType.MESH,
        )

    sent = []

    def send(source, block, target, target_ref=None):
        target_ref = place(block) if target_ref is None else target_ref
        copy = remote(source, target_ref, send_sem.at[len(sent)], recv_sem.at[block], target)
        copy.start()
        sent.append(copy)

    def arrived(block, ref=None):
        ref = place(block) if ref is None else ref
        remote(ref, ref, send_sem.at[0], recv_sem.at[block], twin).wait_recv()

    greet([side, twin, diag] + peers)
    landing = stage if mode == "exchange" else place(side)
    send(in_ref, me, side, stage if mode == "exchange" else None)
    bulk = []
    for slot in range(2 * CAP):
        bulk.append(
            remote(
                far_ref.at[slot, pl.ds(first, heads)],
                got_ref.at[slot],
                bulk_send.at[slot],
                bulk_recv.at[slot],
                side if slot < CAP else diag,
            )
        )
    if near:
        bulk.append(
            remote(
                one_ref, got_one_ref, bulk_send.at[2 * CAP], bulk_recv.at[2 * CAP], twin
            )
        )
    for other in levels:
        send(part(in_ref, other), me, other * 4 + member)
    send(part(in_ref, my_level), me, twin)
    for copy in bulk:
        copy.start()
    own = pltpu.make_async_copy(part(in_ref, my_level), place(me), own_sem.at[0])
    own.start()
    arrived(side, landing)
    for other in levels:
        send(part(landing, other), side, other * 4 + member)
    send(part(landing, my_level), side, twin)
    if mode == "exchange":
        extra = pltpu.make_async_copy(part(stage, my_level), place(side), own_sem.at[1])
        extra.start()
    for peer in peers + side_peers:
        arrived(peer)
        send(place(peer), peer, twin)
    arrived(twin)
    arrived(diag)
    for other in levels:
        arrived(other * 4 + twin_member)
        arrived(other * 4 + diag_member)
    own.wait()
    if mode == "exchange":
        extra.wait()
    for copy in sent:
        copy.wait_send()
    for copy in bulk:
        copy.wait()


def spread(block, far, one, count, spans, mode, first, heads, out_shape, identity, name):
    near = one is not None
    got = jax.ShapeDtypeStruct((far.shape[0], heads) + far.shape[2:], far.dtype)
    outs = (jax.ShapeDtypeStruct(out_shape, block.dtype), got)
    operands = (block, far)
    if near:
        outs = outs + (jax.ShapeDtypeStruct(one.shape, one.dtype),)
        operands = operands + (one,)
    return pl.pallas_call(
        functools.partial(spread_kernel, count, spans, mode, first, heads, near),
        out_shape=outs,
        in_specs=[VM] + [ANY] * (len(operands) - 1),
        out_specs=(VM,) + (ANY,) * (len(outs) - 1),
        scratch_shapes=[
            pltpu.VMEM(block.shape if mode == "exchange" else (16, 128), block.dtype),
            pltpu.SemaphoreType.DMA((count - 1,)),
            pltpu.SemaphoreType.DMA((count,)),
            pltpu.SemaphoreType.DMA((2,)),
            pltpu.SemaphoreType.DMA((2 * CAP + 1,)),
            pltpu.SemaphoreType.DMA((2 * CAP + 1,)),
        ],
        compiler_params=pltpu.CompilerParams(collective_id=identity, has_side_effects=True),
        name=name,
    )(*operands)


def read_kernel(
    head_size, bias_ref, qkv_ref, state_ref, weight_ref, gain_ref, owner_ref, slot_ref, out_ref
):
    step = pl.program_id(0)
    group = qkv_ref.shape[0]
    masks = [owner_ref[:, p : p + 1] > 0 for p in range(state_ref.shape[0])]
    for head in range(group):
        block = qkv_ref[head]
        q_half = block[:, :head_size]
        queries = q_half.astype(jnp.float32)
        keys = block[:, head_size : 2 * head_size].astype(jnp.float32)
        values = block[:, 2 * head_size :].astype(jnp.float32)
        logit = jnp.sum(keys * weight_ref[head], axis=-1, keepdims=True) / math.sqrt(head_size)
        decay = jax.nn.sigmoid(logit + bias_ref[step * group + head])
        unit = keys * lax.rsqrt(jnp.sum(keys * keys, axis=-1, keepdims=True) + 1e-06)
        spreadq = jnp.concatenate(
            [jnp.where(mask, queries, 0.0).astype(jnp.bfloat16) for mask in masks], axis=1
        )
        stacked = state_ref[:, head].reshape(state_ref.shape[0] * head_size, head_size)
        total = jnp.dot(spreadq, stacked, preferred_element_type=jnp.float32)
        readout = decay * total + jnp.sum(queries * unit, axis=-1, keepdims=True) * values
        scaled = readout * lax.rsqrt(jnp.mean(readout * readout, axis=-1, keepdims=True) + 1e-05)
        normed = (scaled * gain_ref[head]).astype(jnp.bfloat16)
        picked = jnp.dot(slot_ref[...], normed, preferred_element_type=jnp.float32)
        out_ref[:, head * head_size : (head + 1) * head_size] = picked.astype(jnp.bfloat16)


def read(qkv, states, gate_weight, gate_bias, norm_gain, owner, slot_pick):
    heads, beams, triple = qkv.shape
    row_local, _, head_size, _ = states.shape
    slots = slot_pick.shape[0]
    group = 4 if heads % 4 == 0 else 1
    return pl.pallas_call(
        functools.partial(read_kernel, head_size),
        grid=(heads // group,),
        out_shape=jax.ShapeDtypeStruct((slots, heads * head_size), jnp.bfloat16),
        in_specs=[
            SM,
            pl.BlockSpec((group, beams, triple), lambda h: (h, 0, 0)),
            pl.BlockSpec((row_local, group, head_size, head_size), lambda h: (0, h, 0, 0)),
            pl.BlockSpec((group, 1, head_size), lambda h: (h, 0, 0)),
            pl.BlockSpec((group, 1, head_size), lambda h: (h, 0, 0)),
            pl.BlockSpec((beams, row_local), lambda h: (0, 0)),
            pl.BlockSpec((slots, beams), lambda h: (0, 0)),
        ],
        out_specs=pl.BlockSpec((slots, group * head_size), lambda h: (0, h)),
        cost_estimate=pl.CostEstimate(
            flops=2 * beams * math.prod(states.shape),
            bytes_accessed=2 * math.prod(states.shape),
            transcendentals=0,
        ),
        name="read_heads",
    )(
        gate_bias,
        qkv,
        states,
        gate_weight.reshape(heads, 1, head_size),
        norm_gain.reshape(heads, 1, head_size),
        owner,
        slot_pick,
    )


def update_kernel(cuts, kind_ref, index_ref, decay_ref, state_ref, one_ref, *refs):
    pieces = refs[: len(cuts)]
    unit_ref, value_ref, out_ref, old, new, in_sem, out_sem = refs[len(cuts) :]
    row_local, heads = old.shape[0], old.shape[1]
    for row in range(row_local):
        @pl.when(kind_ref[row] == 0)
        def _():
            pltpu.make_async_copy(
                state_ref.at[index_ref[row]], old.at[row], in_sem.at[row]
            ).start()

        @pl.when(kind_ref[row] == 1)
        def _():
            pltpu.make_async_copy(one_ref.at[index_ref[row]], old.at[row], in_sem.at[row]).start()

        @pl.when(kind_ref[row] > 1)
        def _():
            slot = (kind_ref[row] - 2) * CAP + index_ref[row]
            for (first, span), piece in zip(cuts, pieces):
                pltpu.make_async_copy(
                    piece.at[slot], old.at[row, pl.ds(first, span)], in_sem.at[row]
                ).start()

    def step(row, carry):
        pltpu.make_async_copy(state_ref.at[0], old.at[row], in_sem.at[row]).wait()
        columns = unit_ref[row]
        values = value_ref[row]
        for head in range(heads):
            fresh = columns[:, head : head + 1] * values[head : head + 1, :]
            prior = old[row, head].astype(jnp.float32)
            new[row, head] = (decay_ref[row, head] * prior + fresh).astype(jnp.bfloat16)
        pltpu.make_async_copy(new.at[row], out_ref.at[row], out_sem.at[row]).start()
        return carry

    lax.fori_loop(0, row_local, step, 0)
    for row in range(row_local):
        pltpu.make_async_copy(new.at[row], out_ref.at[row], out_sem.at[row]).wait()


def update(cuts, kind, index, decay, states, one, pieces, unit, values):
    row_local = states.shape[0]
    return pl.pallas_call(
        functools.partial(update_kernel, cuts),
        out_shape=jax.ShapeDtypeStruct(states.shape, states.dtype),
        in_specs=[SM, SM, SM, ANY, ANY] + [ANY] * len(pieces) + [VM, VM],
        out_specs=ANY,
        scratch_shapes=[
            pltpu.VMEM(states.shape, states.dtype),
            pltpu.VMEM(states.shape, states.dtype),
            pltpu.SemaphoreType.DMA((row_local,)),
            pltpu.SemaphoreType.DMA((row_local,)),
        ],
        cost_estimate=pl.CostEstimate(
            flops=4 * math.prod(states.shape),
            bytes_accessed=4 * math.prod(states.shape),
            transcendentals=0,
        ),
        name="update_states",
    )(kind, index, decay, states, one, *pieces, unit, values)


def fast(
    token_ids, parents, states, embed_table, qkv_weight, gate_weight, gate_bias, norm_gain,
    out_weight
):
    row_local, heads, head_size, _ = states.shape
    width = heads * head_size
    column_local = embed_table.shape[1]
    row_total = token_ids.shape[1]
    users, beams = parents.shape[1], parents.shape[2]
    count = lax.axis_size("rows")
    device = lax.axis_index("rows")
    member, user = device % 4, device // 4
    slots = 16 * ((row_local + 3 * CAP + 15) // 16)

    lists = parents[0]
    owner_block = lists // row_local
    blocks = owner_block.reshape(users, 4, row_local)
    at = jnp.arange(row_local, dtype=jnp.int32)
    same = (blocks[..., :, None] == blocks[..., None, :]) & (at[:, None] > at[None, :])
    rank = jnp.sum(same.astype(jnp.int32), axis=-1)
    offset = jnp.bitwise_xor(blocks, jnp.arange(4, dtype=jnp.int32)[None, :, None])
    slot = jnp.where(offset == 0, at[None, None, :], row_local + (offset - 1) * CAP + rank)
    slot = slot.reshape(users, beams)
    my_list = lax.dynamic_index_in_dim(lists, user, 0, keepdims=False)
    my_slot = lax.dynamic_index_in_dim(slot, user, 0, keepdims=False)
    held = my_list // row_local == member
    within = my_list % row_local
    slot_pick = held[None, :] & (my_slot[None, :] == jnp.arange(slots, dtype=jnp.int32)[:, None])
    owner = (held[:, None] & (within[:, None] == at[None, :])).astype(jnp.float32)
    own_slot = lax.dynamic_slice_in_dim(my_slot, member * row_local, row_local, 0)
    own_within = lax.dynamic_slice_in_dim(within, member * row_local, row_local, 0)
    far = own_slot >= row_local
    kind = jnp.where(far, (own_slot - row_local) // CAP + 1, 0)
    index = jnp.where(far, (own_slot - row_local) % CAP, own_within)

    edges = [0, heads * 3 // 16, heads * 8 // 16, heads]
    cuts = tuple((low, high - low) for low, high in zip(edges, edges[1:]))
    one, far, local_columns = gather(parents, token_ids, states, embed_table)
    every_input, piece_a = spread(
        local_columns, far, None, count, column_local, "columns", *cuts[0],
        (row_total, count * column_local), 1, "spread_inputs"
    )
    projected = jnp.dot(
        every_input,
        qkv_weight.reshape(qkv_weight.shape[0], 3 * column_local),
        preferred_element_type=jnp.float32,
    ).astype(jnp.bfloat16)
    qkv, piece_b, got_one = spread(
        projected.reshape(row_total, 3 * column_local), far, one, count, beams, "exchange",
        *cuts[1], (count * beams, 3 * column_local), 2, "spread_heads"
    )
    qkv = qkv.reshape(count, beams, 3 * column_local)
    normed = read(
        qkv, states, gate_weight, gate_bias, norm_gain, owner, slot_pick.astype(jnp.bfloat16)
    )
    every_normed, piece_c = spread(
        normed, far, None, count, slots, "rows", *cuts[2], (count * slots, width), 3,
        "spread_normed"
    )
    source = (
        (jnp.arange(users, dtype=jnp.int32)[:, None] * 4 + owner_block) * slots + slot
    ).reshape(row_total)
    pick = (source[:, None] == jnp.arange(count * slots, dtype=jnp.int32)[None, :]).astype(
        jnp.bfloat16
    )
    ordered = jnp.dot(pick, every_normed, preferred_element_type=jnp.float32)
    attention = jnp.dot(
        ordered.astype(jnp.bfloat16), out_weight, preferred_element_type=jnp.float32
    )
    layer_out = (local_columns.astype(jnp.float32) + attention).astype(jnp.bfloat16)

    mine = lax.dynamic_slice_in_dim(qkv, member * row_local, row_local, 1)
    keys = mine[:, :, head_size : 2 * head_size].astype(jnp.float32)
    values = jnp.swapaxes(mine[:, :, 2 * head_size :].astype(jnp.float32), 0, 1)
    logit = jnp.sum(keys * gate_weight[:, None, :], axis=-1) / math.sqrt(head_size)
    decay = jax.nn.sigmoid(logit + gate_bias[:, None]).T
    unit = keys * lax.rsqrt(jnp.sum(keys * keys, axis=-1, keepdims=True) + 1e-06)
    state_now = update(
        cuts, kind, index, decay, states, got_one, (piece_a, piece_b, piece_c),
        jnp.transpose(unit, (1, 2, 0)), values
    )
    return (layer_out[None], state_now)


def from_partner(block, axis, stride):
    count = lax.axis_size(axis)
    route = []
    for low in range(count):
        high = low | 1 << stride
        if high != low and high < count:
            route += [(low, high), (high, low)]
    return lax.ppermute(block, axis, route)


def outgoing(state_now, parent_list, member, row_local, partner):
    target = jnp.bitwise_xor(member, partner)
    children = lax.dynamic_slice_in_dim(parent_list, target * row_local, row_local, 0)
    needed = children // row_local == member
    rank_index = jnp.cumsum(needed.astype(jnp.int32)) - 1
    slot_ids = jnp.arange(CAP, dtype=jnp.int32)
    chosen = jnp.sum(
        jnp.where(
            needed[None, :] & (rank_index[None, :] == slot_ids[:, None]),
            (children % row_local)[None, :],
            0,
        ),
        axis=1,
    )
    return jnp.take(state_now, chosen, axis=0)


def route(state_now, parent_list, member, row_local):
    first_out = outgoing(state_now, parent_list, member, row_local, 1)
    second_out = outgoing(state_now, parent_list, member, row_local, 2)
    corner_out = outgoing(state_now, parent_list, member, row_local, 3)
    got_one = from_partner(first_out, "rows", 0)
    got_two = from_partner(second_out, "rows", 1)
    relayed = from_partner(corner_out, "rows", 0)
    got_three = from_partner(relayed, "rows", 1)
    own_list = lax.dynamic_slice_in_dim(parent_list, member * row_local, row_local, 0)
    source = own_list // row_local
    partner = jnp.bitwise_xor(source, member)
    slot_index = jnp.arange(row_local, dtype=jnp.int32)
    earlier = (source[:, None] == source[None, :]) & (slot_index[:, None] > slot_index[None, :])
    rank_index = jnp.sum(earlier.astype(jnp.int32), axis=1)
    position = jnp.where(
        partner == 0, own_list % row_local, row_local + (partner - 1) * CAP + rank_index
    )
    pooled = jnp.concatenate([state_now, got_one, got_two, got_three], 0)
    return jnp.take(pooled, position, axis=0)


def per_device(
    token_ids,
    parents,
    states,
    embed_table,
    qkv_weight,
    gate_weight,
    gate_bias,
    norm_gain,
    out_weight,
):
    row_local = states.shape[0]
    heads = states.shape[1]
    head_size = states.shape[2]
    count = lax.axis_size("rows")
    if (
        embed_table.shape[1] == head_size
        and head_size % 128 == 0
        and count == heads
        and parents.shape[0] == 1
        and parents.shape[2] == 4 * row_local
        and parents.shape[1] * 4 == count
        and parents.shape[2] % 16 == 0
    ):
        return fast(
            token_ids, parents, states, embed_table, qkv_weight, gate_weight, gate_bias,
            norm_gain, out_weight
        )
    width = heads * head_size
    column_local = embed_table.shape[1]
    row_total = token_ids.shape[1]
    device = lax.axis_index("rows")
    member = device % 4
    user_index = device // 4
    weight_flat = qkv_weight.reshape(qkv_weight.shape[0], 3 * column_local)
    local_columns = jnp.take(embed_table, token_ids, axis=0)
    every_proj = jnp.einsum(
        "...rc,cf->...rf",
        lax.all_gather(local_columns, "rows", axis=2, tiled=True),
        weight_flat,
        preferred_element_type=jnp.float32,
    )
    state_now = states
    step_proj = every_proj[0]
    projected = step_proj.astype(jnp.bfloat16).reshape(row_total, 3, column_local)
    mine = lax.all_to_all(projected, "rows", split_axis=0, concat_axis=2, tiled=True)
    queries = mine[:, 0].reshape(row_local, heads, head_size)
    key_float = mine[:, 1].reshape(row_local, heads, head_size).astype(jnp.float32)
    values = mine[:, 2].reshape(row_local, heads, head_size).astype(jnp.float32)
    gate_logit = jnp.sum(key_float * gate_weight, axis=-1) / math.sqrt(head_size) + gate_bias
    decay_rate = jax.nn.sigmoid(gate_logit)
    key_unit = key_float * lax.rsqrt(jnp.sum(key_float * key_float, axis=-1, keepdims=True) + 1e-06)
    parent_list = lax.dynamic_index_in_dim(parents[0], user_index, 0, keepdims=False)
    prior_state = route(state_now, parent_list, member, row_local)
    new_state = (
        decay_rate[:, :, None, None] * prior_state.astype(jnp.float32)
        + key_unit[:, :, :, None] * values[:, :, None, :]
    )
    state_now = new_state.astype(jnp.bfloat16)
    readout = jnp.einsum("rhd,rhde->rhe", queries, state_now, preferred_element_type=jnp.float32)
    scaled = readout * lax.rsqrt(jnp.mean(readout * readout, axis=-1, keepdims=True) + 1e-05)
    normed = (scaled.reshape(row_local, width) * norm_gain).astype(jnp.bfloat16)
    attention = jnp.dot(
        lax.all_gather(normed, "rows", axis=0, tiled=True),
        out_weight,
        preferred_element_type=jnp.float32,
    )
    outputs = [(local_columns[0].astype(jnp.float32) + attention).astype(jnp.bfloat16)]
    return (jnp.stack(outputs), state_now)


def solution(mesh):
    placed = (
        P(None, "groups"),
        P(None, "groups", None),
        P(("groups", "rows"), None, None, None),
        P(None, "rows"),
        P(None, None, "rows"),
        P(),
        P(),
        P(),
        P(None, "rows"),
    )
    return jax.shard_map(
        per_device,
        mesh=mesh,
        in_specs=placed,
        out_specs=(P(None, "groups", "rows"), P(("groups", "rows"), None, None, None)),
        check_vma=False,
    )
```

time: 126 us -> 104 us (0.83); the launches traced: 126 us -> 102 us
  Pallas kernels: 107 us -> 85.5 us
  starting transfers between devices: 3.34 us -> 0 us
    pallas_call x7 -> x6, Pallas kernels: 107 us -> 85.5 us  [the longest x3 67.6 us: spread(): pl.pallas_call(functools.partial(spread_kernel, count, spans, mode, first...]
    ppermute x3 -> x0, starting transfers between devices: 3.34 us -> none  [swap(): lax.ppermute(block, 'rows', [(low, low ^ partner) for low in range(count)])]
  transfers between devices with their start and end apart: 3 -> 0, of which waited for: 0 -> 0; matrix products, arithmetic and copies ran while one was open for 8% -> 0% of each run, Pallas kernels for 77% -> 0%
where the time goes in v2:
time: 104 us; the launch traced here: 102 us
  Pallas kernels  85.5 us (82%)
  local copies, waits for them, and re-layouts  5.81 us (6%)
  other arithmetic  5.18 us (5%)
  matrix products  4.6 us (4%)
    pallas_call x3, Pallas kernels, spread(): pl.pallas_call(functools.partial(spread_kernel, count, spans, mode, first...  67.6 us
    pallas_call x1, Pallas kernels, read(): pl.pallas_call(functools.partial(read_kernel, head_size), grid=(heads //...  6.79 us
    pallas_call x1, Pallas kernels, update(): pl.pallas_call(functools.partial(update_kernel, cuts), out_shape=jax.Shap...  5.95 us
    pallas_call x1, Pallas kernels, gather(): pl.pallas_call(functools.partial(gather_kernel, parents.shape[1]), out_sh...  5.14 us
    dot_general x1, matrix products, fast(): jnp.dot(ordered.astype(jnp.bfloat16), out_weight, preferred_element_type=...  2.33 us
    dot_general x1, matrix products, fast(): jnp.dot(every_input, qkv_weight.reshape(qkv_weight.shape[0], 3 * column_l...  2.27 us

profile of v2, /device:TPU:0, one launch (start us, length us, event | category | flops | bytes accessed | tf_op | source)
XLA Modules:
  0.0 101.9 jit_solution(9121292411399858059)
XLA Ops:
  0.6 0.0 copy-start
  0.7 0.8 squeeze.12
  1.5 0.7 fusion.22
  2.2 0.1 add.144
  2.3 0.1 add.145
  2.4 0.1 broadcast_in_dim.42
  2.5 0.1 broadcast_in_dim.44
  2.6 0.1 xor.28
  2.7 0.1 xor.30
  2.7 0.8 squeeze.13
  3.5 0.4 convert_reduce_fusion
  4.0 0.1 reduce_sum.32
  4.1 0.1 reduce_sum.33
  4.2 0.7 add_select_fusion.2
  4.9 0.6 bitcast_select_fusion
  5.5 0.6 fusion.14.slot_ref
  6.1 0.7 fusion.10.owner_ref
  6.8 1.7 %copy.16 = bf16[2048,3,128]{0,2,1:T(8,128)(2,1)S(1)} copy(bf16[2048,3,128]{2,0,1:T(8,128)(2,1)} %param.13) | data formatting | bytes 3145728 | tf_op args[4]
  8.5 5.1 %gather_rows.1 = (bf16[2,16,128,128]{3,2,1,0:T(8,128)(2,1)}, bf16[4,16,128,128]{3,2,1,0:T(8,128)(2,1)}, bf16[128,128]{1,0:T(8,128)(2,1)}) custom-call(s32[1,4,32]{2,1,0:T(4,128)} %list_ref.1, s32[1,128]{1,0:T(1,128)} %tok_ref.1, bf16[8,16,128,128]{3,2,1,0:T(8,128)(2,1)} %state_ref.5, bf16[4096,8,128]{2,1,0:T(8,128)(2,1)} %bitcast.64), custom_call_target="tpu_custom_call" | custom-call | bytes 6291456 | tf_op jit(solution)/shard_map/gather_rows/pallas_call | solution.py:69
  13.6 16.5 %spread_inputs.1 = (bf16[128,2048]{1,0:T(8,128)(2,1)}, bf16[4,3,128,128]{3,2,1,0:T(8,128)(2,1)}) custom-call(bf16[128,128]{1,0:T(8,128)(2,1)} %get-tuple-element.12.refs_0_, bf16[4,16,128,128]{3,2,1,0:T(8,128)(2,1)} %get-tuple-element.13.refs_1_), custom_call_target="tpu_custom_call" | custom-call | tf_op jit(solution)/shard_map/spread_inputs/pallas_call | solution.py:213
  30.2 2.3 %convolution_convert_fusion.1.refs_0_ = bf16[128,384]{1,0:T(8,128)(2,1)} fusion(bf16[128,2048]{1,0:T(8,128)(2,1)} %get-tuple-element.14, bf16[2048,384]{0,1:T(8,128)(2,1)S(1)} %bitcast.65), kind=kOutput, calls=%fused_computation.2 | convolution fusion | flops 201375744 | bytes 2195456 | tf_op jit(solution)/shard_map/dot_general | solution.py:397
  32.5 22.4 %spread_heads.1 = (bf16[512,384]{1,0:T(8,128)(2,1)}, bf16[4,5,128,128]{3,2,1,0:T(8,128)(2,1)}, bf16[2,16,128,128]{3,2,1,0:T(8,128)(2,1)}) custom-call(bf16[128,384]{1,0:T(8,128)(2,1)} %convolution_convert_fusion.1.refs_0_, bf16[4,16,128,128]{3,2,1,0:T(8,128)(2,1)} %get-tuple-element.13.refs_1_, bf16[2,16,128,128]{3,2,1,0:T(8,128)(2,1)} %get-tuple-element.15.refs_2_), custom_call_target="tpu_custom_call" | custom-call | tf_op jit(solution)/shard_map/spread_heads/pallas_call | solution.py:213
  54.9 6.8 %read_heads.1.refs_0_ = bf16[16,2048]{1,0:T(8,128)(2,1)} custom-call(f32[16]{0:T(128)} %bias_ref.1, bf16[16,32,384]{2,1,0:T(8,128)(2,1)} %bitcast.66, bf16[8,16,128,128]{3,2,1,0:T(8,128)(2,1)} %state_ref.5, f32[16,1,128]{2,1,0:T(1,128)} %bitcast.68, f32[16,1,128]{2,1,0:T(1,128)} %bitcast.69, f32[32,8]{1,0:T(8,128)} %fusion.10.owner_ref, ...), custom_call_target="tpu_custom_call" | custom-call | flops 134217728 | bytes 4194304 | tf_op jit(solution)/shard_map/read_heads/pallas_call | solution.py:263
  61.7 0.0 copy-start.1
  61.7 0.8 constant_dynamic-slice_fusion.1
  62.5 0.0 copy-start.2
  62.5 0.0 copy-start.3
  62.5 28.6 %spread_normed.1 = (bf16[256,2048]{1,0:T(8,128)(2,1)}, bf16[4,8,128,128]{3,2,1,0:T(8,128)(2,1)}) custom-call(bf16[16,2048]{1,0:T(8,128)(2,1)} %read_heads.1.refs_0_, bf16[4,16,128,128]{3,2,1,0:T(8,128)(2,1)} %get-tuple-element.13.refs_1_), custom_call_target="tpu_custom_call" | custom-call | tf_op jit(solution)/shard_map/spread_normed/pallas_call | solution.py:213
  91.2 0.0 copy-done
  91.2 0.0 copy-done.1
  91.2 2.3 %fusion.3 = bf16[1,128,128]{2,1,0:T(8,128)(2,1)} fusion(bf16[2048,128]{1,0:T(8,128)(2,1)S(1)} %copy-done, bf16[256,2048]{1,0:T(8,128)(2,1)} %get-tuple-element.17, s32[128]{0:T(128)S(1)} %fusion.21, bf16[128,128]{1,0:T(8,128)(2,1)S(1)} %copy-done.1), kind=kOutput, calls=%fused_computation.5 | convolution fusion | flops 201670656 | bytes 1638912 | tf_op jit(solution)/shard_map/dot_general | solution.py:421
  93.5 0.0 copy-done.2
  93.5 0.1 fusion.5
  93.6 0.0 copy-done.3
  93.6 0.6 divide_bitcast_fusion
  94.3 0.1 fusion.6
  94.3 0.6 convert_bitcast_fusion.refs_4_
  95.0 1.0 copy.18.refs_3_
  96.0 6.0 %update_states.1 = bf16[8,16,128,128]{3,2,1,0:T(8,128)(2,1)} custom-call(s32[8]{0:T(128)} %get-tuple-element.29.kind_ref, s32[8]{0:T(128)} %get-tuple-element.28.index_ref, f32[8,16]{1,0:T(8,128)} %get-tuple-element.30.decay_ref, bf16[8,16,128,128]{3,2,1,0:T(8,128)(2,1)} %state_ref.5, bf16[2,16,128,128]{3,2,1,0:T(8,128)(2,1)} %get-tuple-element.18.one_ref, ...), custom_call_target="tpu_custom_call" | custom-call | flops 8388608 | bytes 8388608 | tf_op jit(solution)/shard_map/update_states/pallas_call | solution.py:335
  (10 shorter events, 0.1 us)
Async XLA Ops:
  0.6 90.5 %copy-start = (bf16[2048,128]{1,0:T(8,128)(2,1)S(1)}, bf16[2048,128]{1,0:T(8,128)(2,1)}, u32[]{:S(2)}) copy-start(bf16[2048,128]{1,0:T(8,128)(2,1)} %param.17) | copy-start | bytes 1572868
  61.7 29.5 %copy-start.1 = (bf16[128,128]{1,0:T(8,128)(2,1)S(1)}, bf16[128,128]{1,0:T(8,128)(2,1)}, u32[]{:S(2)}) copy-start(bf16[128,128]{1,0:T(8,128)(2,1)} %get-tuple-element.12.refs_0_) | copy-start | bytes 98308
  62.5 31.0 %copy-start.2 = (f32[16,128]{1,0:T(8,128)S(1)}, f32[16,128]{1,0:T(8,128)}, u32[]{:S(2)}) copy-start(f32[16,128]{1,0:T(8,128)} %param.14) | copy-start | bytes 24580
  62.5 31.1 %copy-start.3 = (f32[16]{0:T(128)S(1)}, f32[16]{0:T(128)}, u32[]{:S(2)}) copy-start(f32[16]{0:T(128)} %bias_ref.1) | copy-start | bytes 196

commit v3 on v2

--- a/solution.py
+++ b/solution.py
@@ -9,14 +9,15 @@
 from jax.sharding import PartitionSpec as P
 
 CAP = 2
+AHEAD, BEHIND, MIDDLE = 2, 3, 4
 ANY = pl.BlockSpec(memory_space=pl.ANY)
 VM = pl.BlockSpec(memory_space=pltpu.VMEM)
 SM = pl.BlockSpec(memory_space=pltpu.SMEM)
 
 
 def gather_kernel(
-    level, list_ref, tok_ref, state_ref, table_ref, one_ref, far_ref, out_ref,
-    buf, rows_in, wide, rows_out, in_sem, out_sem, row_sem
+    middle, list_ref, tok_ref, state_ref, table_ref, one_ref, far_ref, two_ref, three_ref, out_ref,
+    buf, rows_in, wide, rows_out, in_sem, out_sem, row_sem, mid_sem
 ):
     device = lax.axis_index("rows")
     member, user = device % 4, device // 4
@@ -48,6 +49,13 @@
         store = pltpu.make_async_copy(buf.at[slot], target, out_sem.at[slot])
         store.start()
         stores.append(store)
+        if slot >= CAP:
+            half = (two_ref, three_ref)[slot // CAP - 1]
+            store = pltpu.make_async_copy(
+                buf.at[slot, pl.ds(*middle)], half.at[slot % CAP], mid_sem.at[slot - CAP]
+            )
+            store.start()
+            stores.append(store)
     pltpu.make_async_copy(table_ref.at[pl.ds(0, count)], rows_in, row_sem).wait()
     wide[...] = rows_in[...].astype(jnp.float32).reshape(wide.shape)
 
@@ -61,20 +69,22 @@
         store.wait()
 
 
-def gather(parents, tokens, states, table):
+def gather(middle, parents, tokens, states, table):
     rest = states.shape[1:]
     slots = 3 * CAP
     count, width = tokens.shape[1], table.shape[1]
     size = slots * math.prod(rest) * 2
     return pl.pallas_call(
-        functools.partial(gather_kernel, parents.shape[1]),
+        functools.partial(gather_kernel, middle),
         out_shape=(
             jax.ShapeDtypeStruct((CAP,) + rest, states.dtype),
             jax.ShapeDtypeStruct((2 * CAP,) + rest, states.dtype),
+            jax.ShapeDtypeStruct((CAP, middle[1]) + rest[1:], states.dtype),
+            jax.ShapeDtypeStruct((CAP, middle[1]) + rest[1:], states.dtype),
             jax.ShapeDtypeStruct((count, width), table.dtype),
         ),
         in_specs=[SM, SM, ANY, ANY],
-        out_specs=(ANY, ANY, VM),
+        out_specs=(ANY, ANY, ANY, ANY, VM),
         scratch_shapes=[
             pltpu.VMEM((slots,) + rest, states.dtype),
             pltpu.VMEM((count, 8, width), table.dtype),
@@ -83,6 +93,7 @@
             pltpu.SemaphoreType.DMA((slots,)),
             pltpu.SemaphoreType.DMA((slots,)),
             pltpu.SemaphoreType.DMA,
+            pltpu.SemaphoreType.DMA((2 * CAP,)),
         ],
         cost_estimate=pl.CostEstimate(flops=0, bytes_accessed=2 * size, transcendentals=0),
         name="gather_rows",
@@ -98,24 +109,31 @@
     pl.semaphore_wait(barrier, len(peers))
 
 
-def spread_kernel(count, spans, mode, first, heads, near, *refs):
-    refs = list(refs)
-    in_ref, far_ref = refs[0], refs[1]
-    one_ref = refs.pop(2) if near else None
-    out_ref, got_ref = refs[2], refs[3]
-    got_one_ref = refs.pop(4) if near else None
-    stage, send_sem, recv_sem, own_sem, bulk_send, bulk_recv = refs[4:]
+def remote(source, target_ref, out_sem, in_sem, target):
+    return pltpu.make_async_remote_copy(
+        src_ref=source,
+        dst_ref=target_ref,
+        send_sem=out_sem,
+        recv_sem=in_sem,
+        device_id={"rows": target},
+        device_id_type=pl.DeviceIdType.MESH,
+    )
+
+
+def neighbours(count):
     me = lax.axis_index("rows")
-    level = count // 4
-    member = me % 4
-    my_level = me // 4
+    member, my_level = me % 4, me // 4
     side_member = (member + 2) % 4
     twin_member = member + 1 - 2 * (member % 2)
     diag_member = (twin_member + 2) % 4
-    side = my_level * 4 + side_member
-    twin = my_level * 4 + twin_member
-    diag = my_level * 4 + diag_member
-    levels = [(my_level + k) % level for k in range(1, level)]
+    levels = [(my_level + k) % (count // 4) for k in range(1, count // 4)]
+    return me, my_level, member, side_member, twin_member, diag_member, levels
+
+
+def phase(count, spans, mode, in_ref, out_ref, stage, sems, bulk):
+    send_sem, recv_sem, own_sem = sems
+    me, my_level, member, side_member, twin_member, diag_member, levels = neighbours(count)
+    side, twin, diag = (my_level * 4 + m for m in (side_member, twin_member, diag_member))
     peers = [other * 4 + member for other in levels]
     side_peers = [other * 4 + side_member for other in levels]
 
@@ -128,16 +146,6 @@
         if mode == "exchange":
             return ref.at[pl.ds(pl.multiple_of(other * spans, spans), spans)]
         return ref
-
-    def remote(source, target_ref, out_sem, in_sem, target):
-        return pltpu.make_async_remote_copy(
-            src_ref=source,
-            dst_ref=target_ref,
-            send_sem=out_sem,
-            recv_sem=in_sem,
-            device_id={"rows": target},
-            device_id_type=pl.DeviceIdType.MESH,
-        )
 
     sent = []
 
@@ -151,26 +159,8 @@
         ref = place(block) if ref is None else ref
         remote(ref, ref, send_sem.at[0], recv_sem.at[block], twin).wait_recv()
 
-    greet([side, twin, diag] + peers)
     landing = stage if mode == "exchange" else place(side)
     send(in_ref, me, side, stage if mode == "exchange" else None)
-    bulk = []
-    for slot in range(2 * CAP):
-        bulk.append(
-            remote(
-                far_ref.at[slot, pl.ds(first, heads)],
-                got_ref.at[slot],
-                bulk_send.at[slot],
-                bulk_recv.at[slot],
-                side if slot < CAP else diag,
-            )
-        )
-    if near:
-        bulk.append(
-            remote(
-                one_ref, got_one_ref, bulk_send.at[2 * CAP], bulk_recv.at[2 * CAP], twin
-            )
-        )
     for other in levels:
         send(part(in_ref, other), me, other * 4 + member)
     send(part(in_ref, my_level), me, twin)
@@ -196,36 +186,132 @@
     own.wait()
     if mode == "exchange":
         extra.wait()
+    return sent
+
+
+def far_copies(count, far_ref, got_ref, first, offset, heads, out_sem, in_sem, at):
+    _, my_level, _, side_member, _, diag_member, _ = neighbours(count)
+    return [
+        remote(
+            far_ref.at[slot, pl.ds(first + offset, heads)],
+            got_ref.at[slot, pl.ds(offset, heads)],
+            out_sem.at[at + slot],
+            in_sem.at[at + slot],
+            my_level * 4 + (side_member if slot < CAP else diag_member),
+        )
+        for slot in range(2 * CAP)
+    ]
+
+
+def meet(count):
+    _, my_level, member, side_member, twin_member, diag_member, levels = neighbours(count)
+    greet(
+        [my_level * 4 + m for m in (side_member, twin_member, diag_member)]
+        + [other * 4 + member for other in levels]
+    )
+
+
+def inputs_kernel(
+    count, beams, split, in_ref, weight_ref, far_ref, one_ref, out_ref, got_ref, got_one_ref,
+    weights, every, proj, stage, weight_sem, send_a, recv_a, own_a, send_b, recv_b, own_b,
+    bulk_send, bulk_recv
+):
+    column_local = in_ref.shape[1]
+    load = pltpu.make_async_copy(weight_ref, weights, weight_sem)
+    load.start()
+    meet(count)
+    _, my_level, _, _, twin_member, _, _ = neighbours(count)
+    ahead = far_copies(count, far_ref, got_ref, 0, 0, split[0], bulk_send, bulk_recv, 0)
+    behind = far_copies(
+        count, far_ref, got_ref, 0, split[0], split[1], bulk_send, bulk_recv, 2 * CAP
+    )
+    behind.append(
+        remote(
+            one_ref, got_one_ref, bulk_send.at[4 * CAP], bulk_recv.at[4 * CAP],
+            my_level * 4 + twin_member,
+        )
+    )
+    sent = phase(
+        count, column_local, "columns", in_ref, every, None, (send_a, recv_a, own_a), ahead
+    )
+    load.wait()
+    for slab in range(3):
+        proj[:, slab * column_local : (slab + 1) * column_local] = jnp.dot(
+            every[...], weights[slab], preferred_element_type=jnp.float32
+        ).astype(jnp.bfloat16)
+    sent += phase(count, beams, "exchange", proj, out_ref, stage, (send_b, recv_b, own_b), behind)
+    for copy in sent:
+        copy.wait_send()
+    for copy in ahead + behind:
+        copy.wait()
+
+
+def inputs(local_columns, weights, far, one, count, beams, split):
+    row_total, column_local = local_columns.shape
+    depth = weights.shape[1]
+    sems = [
+        pltpu.SemaphoreType.DMA((count - 1,)),
+        pltpu.SemaphoreType.DMA((count,)),
+        pltpu.SemaphoreType.DMA((2,)),
+    ]
+    return pl.pallas_call(
+        functools.partial(inputs_kernel, count, beams, split),
+        out_shape=(
+            jax.ShapeDtypeStruct((count * beams, 3 * column_local), jnp.bfloat16),
+            jax.ShapeDtypeStruct((far.shape[0], sum(split)) + far.shape[2:], far.dtype),
+            jax.ShapeDtypeStruct(one.shape, one.dtype),
+        ),
+        in_specs=[VM, ANY, ANY, ANY],
+        out_specs=(VM, ANY, ANY),
+        scratch_shapes=[
+            pltpu.VMEM(weights.shape, weights.dtype),
+            pltpu.VMEM((row_total, depth), jnp.bfloat16),
+            pltpu.VMEM((row_total, 3 * column_local), jnp.bfloat16),
+            pltpu.VMEM((row_total, 3 * column_local), jnp.bfloat16),
+            pltpu.SemaphoreType.DMA,
+        ]
+        + sems
+        + sems
+        + [pltpu.SemaphoreType.DMA((4 * CAP + 1,)), pltpu.SemaphoreType.DMA((4 * CAP + 1,))],
+        compiler_params=pltpu.CompilerParams(collective_id=1, has_side_effects=True),
+        name="spread_inputs",
+    )(local_columns, weights, far, one)
+
+
+def normed_kernel(
+    count, first, heads, in_ref, far_ref, out_ref, got_ref, send_a, recv_a, own_a, bulk_send,
+    bulk_recv
+):
+    meet(count)
+    bulk = far_copies(count, far_ref, got_ref, first, 0, heads, bulk_send, bulk_recv, 0)
+    sent = phase(
+        count, in_ref.shape[0], "rows", in_ref, out_ref, None, (send_a, recv_a, own_a), bulk
+    )
     for copy in sent:
         copy.wait_send()
     for copy in bulk:
         copy.wait()
 
 
-def spread(block, far, one, count, spans, mode, first, heads, out_shape, identity, name):
-    near = one is not None
-    got = jax.ShapeDtypeStruct((far.shape[0], heads) + far.shape[2:], far.dtype)
-    outs = (jax.ShapeDtypeStruct(out_shape, block.dtype), got)
-    operands = (block, far)
-    if near:
-        outs = outs + (jax.ShapeDtypeStruct(one.shape, one.dtype),)
-        operands = operands + (one,)
+def spread_normed(normed, far, count, first, heads):
     return pl.pallas_call(
-        functools.partial(spread_kernel, count, spans, mode, first, heads, near),
-        out_shape=outs,
-        in_specs=[VM] + [ANY] * (len(operands) - 1),
-        out_specs=(VM,) + (ANY,) * (len(outs) - 1),
+        functools.partial(normed_kernel, count, first, heads),
+        out_shape=(
+            jax.ShapeDtypeStruct((count * normed.shape[0], normed.shape[1]), normed.dtype),
+            jax.ShapeDtypeStruct((far.shape[0], heads) + far.shape[2:], far.dtype),
+        ),
+        in_specs=[VM, ANY],
+        out_specs=(VM, ANY),
         scratch_shapes=[
-            pltpu.VMEM(block.shape if mode == "exchange" else (16, 128), block.dtype),
             pltpu.SemaphoreType.DMA((count - 1,)),
             pltpu.SemaphoreType.DMA((count,)),
             pltpu.SemaphoreType.DMA((2,)),
-            pltpu.SemaphoreType.DMA((2 * CAP + 1,)),
-            pltpu.SemaphoreType.DMA((2 * CAP + 1,)),
+            pltpu.SemaphoreType.DMA((2 * CAP,)),
+            pltpu.SemaphoreType.DMA((2 * CAP,)),
         ],
-        compiler_params=pltpu.CompilerParams(collective_id=identity, has_side_effects=True),
-        name=name,
-    )(*operands)
+        compiler_params=pltpu.CompilerParams(collective_id=2, has_side_effects=True),
+        name="spread_normed",
+    )(normed, far)
 
 
 def read_kernel(
@@ -291,9 +377,10 @@
     )
 
 
-def update_kernel(cuts, kind_ref, index_ref, decay_ref, state_ref, one_ref, *refs):
-    pieces = refs[: len(cuts)]
-    unit_ref, value_ref, out_ref, old, new, in_sem, out_sem = refs[len(cuts) :]
+def update_kernel(
+    cuts, kind_ref, index_ref, decay_ref, state_ref, one_ref, two_ref, three_ref, early_ref,
+    late_ref, unit_ref, value_ref, out_ref, old, new, in_sem, out_sem
+):
     row_local, heads = old.shape[0], old.shape[1]
     for row in range(row_local):
         @pl.when(kind_ref[row] == 0)
@@ -309,9 +396,16 @@
         @pl.when(kind_ref[row] > 1)
         def _():
             slot = (kind_ref[row] - 2) * CAP + index_ref[row]
-            for (first, span), piece in zip(cuts, pieces):
+            for cut, piece in ((cuts[0], early_ref), (cuts[2], late_ref)):
                 pltpu.make_async_copy(
-                    piece.at[slot], old.at[row, pl.ds(first, span)], in_sem.at[row]
+                    piece.at[slot], old.at[row, pl.ds(*cut)], in_sem.at[row]
+                ).start()
+
+        for other, piece in ((2, two_ref), (3, three_ref)):
+            @pl.when(kind_ref[row] == other)
+            def _():
+                pltpu.make_async_copy(
+                    piece.at[index_ref[row]], old.at[row, pl.ds(*cuts[1])], in_sem.at[row]
                 ).start()
 
     def step(row, carry):
@@ -330,12 +424,12 @@
         pltpu.make_async_copy(new.at[row], out_ref.at[row], out_sem.at[row]).wait()
 
 
-def update(cuts, kind, index, decay, states, one, pieces, unit, values):
+def update(cuts, kind, index, decay, states, pieces, unit, values):
     row_local = states.shape[0]
     return pl.pallas_call(
         functools.partial(update_kernel, cuts),
         out_shape=jax.ShapeDtypeStruct(states.shape, states.dtype),
-        in_specs=[SM, SM, SM, ANY, ANY] + [ANY] * len(pieces) + [VM, VM],
+        in_specs=[SM, SM, SM, ANY] + [ANY] * len(pieces) + [VM, VM],
         out_specs=ANY,
         scratch_shapes=[
             pltpu.VMEM(states.shape, states.dtype),
@@ -349,7 +443,12 @@
             transcendentals=0,
         ),
         name="update_states",
-    )(kind, index, decay, states, one, *pieces, unit, values)
+    )(kind, index, decay, states, *pieces, unit, values)
+
+
+def swap(block, partner):
+    count = lax.axis_size("rows")
+    return lax.ppermute(block, "rows", [(low, low ^ partner) for low in range(count)])
 
 
 def fast(
@@ -357,7 +456,6 @@
     out_weight
 ):
     row_local, heads, head_size, _ = states.shape
-    width = heads * head_size
     column_local = embed_table.shape[1]
     row_total = token_ids.shape[1]
     users, beams = parents.shape[1], parents.shape[2]
@@ -366,7 +464,21 @@
     member, user = device % 4, device // 4
     slots = 16 * ((row_local + 3 * CAP + 15) // 16)
 
-    lists = parents[0]
+    split = (heads * AHEAD // 16, heads * BEHIND // 16)
+    middle = heads * MIDDLE // 16
+    early = sum(split)
+    cuts = ((0, early), (early, middle), (early + middle, heads - early - middle))
+    one, far, two, three, local_columns = gather(
+        cuts[1], parents, token_ids, states, embed_table
+    )
+    qkv, piece_a, got_one = inputs(
+        local_columns, jnp.transpose(qkv_weight, (1, 0, 2)), far, one, count, beams, split
+    )
+    two, three, qkv, lists = lax.optimization_barrier((two, three, qkv, parents[0]))
+    got_two = swap(two, 2)
+    got_three = swap(three, 3)
+    qkv = qkv.reshape(count, beams, 3 * column_local)
+
     owner_block = lists // row_local
     blocks = owner_block.reshape(users, 4, row_local)
     at = jnp.arange(row_local, dtype=jnp.int32)
@@ -383,55 +495,38 @@
     owner = (held[:, None] & (within[:, None] == at[None, :])).astype(jnp.float32)
     own_slot = lax.dynamic_slice_in_dim(my_slot, member * row_local, row_local, 0)
     own_within = lax.dynamic_slice_in_dim(within, member * row_local, row_local, 0)
-    far = own_slot >= row_local
-    kind = jnp.where(far, (own_slot - row_local) // CAP + 1, 0)
-    index = jnp.where(far, (own_slot - row_local) % CAP, own_within)
-
-    edges = [0, heads * 3 // 16, heads * 8 // 16, heads]
-    cuts = tuple((low, high - low) for low, high in zip(edges, edges[1:]))
-    one, far, local_columns = gather(parents, token_ids, states, embed_table)
-    every_input, piece_a = spread(
-        local_columns, far, None, count, column_local, "columns", *cuts[0],
-        (row_total, count * column_local), 1, "spread_inputs"
-    )
-    projected = jnp.dot(
-        every_input,
-        qkv_weight.reshape(qkv_weight.shape[0], 3 * column_local),
-        preferred_element_type=jnp.float32,
-    ).astype(jnp.bfloat16)
-    qkv, piece_b, got_one = spread(
-        projected.reshape(row_total, 3 * column_local), far, one, count, beams, "exchange",
-        *cuts[1], (count * beams, 3 * column_local), 2, "spread_heads"
-    )
-    qkv = qkv.reshape(count, beams, 3 * column_local)
-    normed = read(
-        qkv, states, gate_weight, gate_bias, norm_gain, owner, slot_pick.astype(jnp.bfloat16)
-    )
-    every_normed, piece_c = spread(
-        normed, far, None, count, slots, "rows", *cuts[2], (count * slots, width), 3,
-        "spread_normed"
-    )
+    far_row = own_slot >= row_local
+    kind = jnp.where(far_row, (own_slot - row_local) // CAP + 1, 0)
+    index = jnp.where(far_row, (own_slot - row_local) % CAP, own_within)
     source = (
         (jnp.arange(users, dtype=jnp.int32)[:, None] * 4 + owner_block) * slots + slot
     ).reshape(row_total)
     pick = (source[:, None] == jnp.arange(count * slots, dtype=jnp.int32)[None, :]).astype(
         jnp.bfloat16
     )
-    ordered = jnp.dot(pick, every_normed, preferred_element_type=jnp.float32)
-    attention = jnp.dot(
-        ordered.astype(jnp.bfloat16), out_weight, preferred_element_type=jnp.float32
-    )
-    layer_out = (local_columns.astype(jnp.float32) + attention).astype(jnp.bfloat16)
-
+
+    normed = read(
+        qkv, states, gate_weight, gate_bias, norm_gain, owner, slot_pick.astype(jnp.bfloat16)
+    )
     mine = lax.dynamic_slice_in_dim(qkv, member * row_local, row_local, 1)
     keys = mine[:, :, head_size : 2 * head_size].astype(jnp.float32)
     values = jnp.swapaxes(mine[:, :, 2 * head_size :].astype(jnp.float32), 0, 1)
     logit = jnp.sum(keys * gate_weight[:, None, :], axis=-1) / math.sqrt(head_size)
     decay = jax.nn.sigmoid(logit + gate_bias[:, None]).T
     unit = keys * lax.rsqrt(jnp.sum(keys * keys, axis=-1, keepdims=True) + 1e-06)
+    unit = jnp.transpose(unit, (1, 2, 0))
+    normed, pick, decay, unit, values, kind, index = lax.optimization_barrier(
+        (normed, pick, decay, unit, values, kind, index)
+    )
+    every_normed, piece_c = spread_normed(normed, far, count, *cuts[2])
+    ordered = jnp.dot(pick, every_normed, preferred_element_type=jnp.float32)
+    attention = jnp.dot(
+        ordered.astype(jnp.bfloat16), out_weight, preferred_element_type=jnp.float32
+    )
+    layer_out = (local_columns.astype(jnp.float32) + attention).astype(jnp.bfloat16)
     state_now = update(
-        cuts, kind, index, decay, states, got_one, (piece_a, piece_b, piece_c),
-        jnp.transpose(unit, (1, 2, 0)), values
+        cuts, kind, index, decay, states,
+        (got_one, got_two, got_three, piece_a, piece_c), unit, values
     )
     return (layer_out[None], state_now)
 

time: 104 us -> 87.2 us (0.84); the launches traced: 102 us -> 86.9 us
  Pallas kernels: 85.5 us -> 75.5 us
  local copies, waits for them, and re-layouts: 5.81 us -> 3.07 us
  matrix products: 4.6 us -> 2.29 us
  other arithmetic: 5.18 us -> 4 us
  starting transfers between devices: 0 us -> 1.16 us
    pallas_call x4 -> x3, Pallas kernels: 72.8 us -> 62.4 us  [the longest x1 28.9 us: spread_normed(): pl.pallas_call(functools.partial(normed_kernel, count, first, heads), out...]
    dot_general x1 -> x0, matrix products: 2.27 us -> none  [fast(): jnp.dot(every_input, qkv_weight.reshape(qkv_weight.shape[0], 3 * column_l...]
    squeeze x2 -> x0, local copies, waits for them, and re-layouts: 1.58 us -> none  [fast(): lists = parents[0]]
    ppermute x0 -> x2, starting transfers between devices: none -> 1.16 us  [swap(): lax.ppermute(block, 'rows', [(low, low ^ partner) for low in range(count)])]
  transfers between devices with their start and end apart: 0 -> 2, of which waited for: 0 -> 0; matrix products, arithmetic and copies ran while one was open for 0% -> 10% of each run, Pallas kernels for 0% -> 41%
where the time goes in v3:
time: 87.2 us; the launch traced here: 86.9 us
  Pallas kernels  75.5 us (87%)
  other arithmetic  4 us (5%)
  local copies, waits for them, and re-layouts  3.07 us (4%)
  matrix products  2.29 us (3%)
  starting transfers between devices  1.16 us (1%)
    pallas_call x1, Pallas kernels, spread_normed(): pl.pallas_call(functools.partial(normed_kernel, count, first, heads), out...  28.9 us
    pallas_call x1, Pallas kernels, inputs(): pl.pallas_call(functools.partial(inputs_kernel, count, beams, split), out...  28.2 us
    pallas_call x1, Pallas kernels, read(): pl.pallas_call(functools.partial(read_kernel, head_size), grid=(heads //...  6.76 us
    pallas_call x1, Pallas kernels, update(): pl.pallas_call(functools.partial(update_kernel, cuts), out_shape=jax.Shap...  6.32 us
    pallas_call x1, Pallas kernels, gather(): pl.pallas_call(functools.partial(gather_kernel, middle), out_shape=(jax.S...  5.41 us
    dot_general x1, matrix products, fast(): jnp.dot(ordered.astype(jnp.bfloat16), out_weight, preferred_element_type=...  2.29 us
  transfers between devices with their start and end apart: 2, of which 0 were waited for; matrix products, arithmetic and copies ran while one was open for 10% of the time, Pallas kernels for 41%

profile of v3, /device:TPU:0, one launch (start us, length us, event | category | flops | bytes accessed | tf_op | source)
XLA Modules:
  0.0 86.9 jit_solution(14785706168798786391)
XLA Ops:
  0.6 0.0 copy-start
  0.6 5.4 %gather_rows.1 = (bf16[2,16,128,128]{3,2,1,0:T(8,128)(2,1)}, bf16[4,16,128,128]{3,2,1,0:T(8,128)(2,1)}, bf16[2,4,128,128]{3,2,1,0:T(8,128)(2,1)}, bf16[2,4,128,128]{3,2,1,0:T(8,128)(2,1)}, bf16[128,128]{1,0:T(8,128)(2,1)}) custom-call(s32[1,4,32]{2,1,0:T(4,128)} %list_ref.1, s32[1,128]{1,0:T(1,128)} %tok_ref.1, bf16[8,16,128,128]{3,2,1,0:T(8,128)(2,1)} %state_ref.5, ...), custom_call_target="tpu_custom_call" | custom-call | bytes 6291456 | tf_op jit(solution)/shard_map/gather_rows/pallas_call | solution.py:77
  6.1 0.0 copy-start.8
  6.1 0.0 copy-start.7
  6.1 0.0 copy-start.5
  6.1 0.0 copy-start.4
  6.1 0.0 copy-start.6
  6.1 28.2 %spread_inputs.1 = (bf16[512,384]{1,0:T(8,128)(2,1)}, bf16[4,5,128,128]{3,2,1,0:T(8,128)(2,1)}, bf16[2,16,128,128]{3,2,1,0:T(8,128)(2,1)}) custom-call(bf16[128,128]{1,0:T(8,128)(2,1)} %get-tuple-element.23.in_ref, bf16[3,2048,128]{2,1,0:T(8,128)(2,1)} %bitcast.56, bf16[4,16,128,128]{3,2,1,0:T(8,128)(2,1)} %get-tuple-element.26.far_ref, ...), custom_call_target="tpu_custom_call" | custom-call | tf_op jit(solution)/shard_map/spread_inputs/pallas_call | solution.py:257
  34.3 0.0 copy-start.3
  34.3 0.0 copy-done.8
  34.3 0.9 %collective-permute-start = (bf16[2,4,128,128]{3,2,1,0:T(8,128)(2,1)S(1)}, bf16[2,4,128,128]{3,2,1,0:T(8,128)(2,1)S(1)}, u32[]{:S(2)}, u32[]{:S(2)}) collective-permute-start(bf16[2,4,128,128]{3,2,1,0:T(8,128)(2,1)S(1)} %copy-done.8), channel_id=1, source_target_pairs={{0,2},{1,3},{2,0},{3,1},{4,6},{5,7},{6,4},{7,5},{8,10},{9,11},{10,... | collective-permute-start | bytes 786440 | tf_op jit(solution)/shard_map/ppermute | solution.py:451
  35.2 0.0 copy-done.7
  35.2 0.3 collective-permute-start.1
  35.5 0.0 copy-done.5
  35.6 0.1 broadcast_in_dim.16
  35.7 0.1 xor.14
  35.7 0.1 eq.92
  35.8 0.4 convert_reduce_fusion
  36.3 0.1 reduce_sum.30
  36.3 0.1 multiply_add_fusion
  36.4 0.1 eq.100
  36.5 0.8 constant_dynamic-slice_fusion.1
  37.3 0.0 copy-done.4
  37.3 0.1 fusion.6
  37.4 0.0 copy-done.6
  37.4 0.6 divide_bitcast_fusion
  38.0 0.1 fusion.7
  38.1 0.6 convert_bitcast_fusion.value_ref
  38.7 0.1 fusion.4
  38.8 0.6 fusion.11.slot_ref
  39.4 0.7 fusion.9.owner_ref
  40.1 6.8 %read_heads.1.in_ref = bf16[16,2048]{1,0:T(8,128)(2,1)} custom-call(f32[16]{0:T(128)} %bias_ref.1, bf16[16,32,384]{2,1,0:T(8,128)(2,1)} %bitcast.58, bf16[8,16,128,128]{3,2,1,0:T(8,128)(2,1)} %state_ref.5, f32[16,1,128]{2,1,0:T(1,128)} %bitcast.59, f32[16,1,128]{2,1,0:T(1,128)} %bitcast.64, f32[32,8]{1,0:T(8,128)} %fusion.9.owner_ref, ...), custom_call_target="tpu_custom_call" | custom-call | flops 134217728 | bytes 4194304 | tf_op jit(solution)/shard_map/read_heads/pallas_call | solution.py:349
  46.9 0.7 bitcast_select_fusion
  47.5 28.9 %spread_normed.1 = (bf16[256,2048]{1,0:T(8,128)(2,1)}, bf16[4,7,128,128]{3,2,1,0:T(8,128)(2,1)}) custom-call(bf16[16,2048]{1,0:T(8,128)(2,1)} %read_heads.1.in_ref, bf16[4,16,128,128]{3,2,1,0:T(8,128)(2,1)} %get-tuple-element.26.far_ref), custom_call_target="tpu_custom_call" | custom-call | tf_op jit(solution)/shard_map/spread_normed/pallas_call | solution.py:297
  76.4 1.0 %copy.16.unit_ref = f32[8,128,16]{2,1,0:T(8,128)} copy(f32[8,128,16]{1,2,0:T(8,128)S(1)} %fusion.7) | data formatting | bytes 131072 | tf_op jit(solution)/shard_map/optimization_barrier | solution.py:518
  77.4 0.0 copy-done
  77.4 0.0 copy-done.3
  77.4 2.3 %fusion.3 = bf16[1,128,128]{2,1,0:T(8,128)(2,1)} fusion(bf16[2048,128]{1,0:T(8,128)(2,1)S(1)} %copy-done, bf16[128,256]{1,0:T(8,128)(2,1)S(1)} %fusion.4, bf16[256,2048]{1,0:T(8,128)(2,1)} %get-tuple-element.33, bf16[128,128]{1,0:T(8,128)(2,1)S(1)} %copy-done.3), kind=kOutput, calls=%fused_computation.4 | convolution fusion | flops 201637888 | bytes 1703936 | tf_op jit(solution)/shard_map/dot_general | solution.py:523
  79.7 0.0 collective-permute-done.two_ref
  79.7 0.0 copy-start.1
  79.7 0.0 collective-permute-done.1.three_ref
  79.7 0.0 copy-start.2
  79.7 0.7 copy-done.1
  80.4 0.1 copy-done.2
  80.5 6.3 %update_states.1 = bf16[8,16,128,128]{3,2,1,0:T(8,128)(2,1)} custom-call(s32[8]{0:T(128)} %get-tuple-element.34.kind_ref, s32[8]{0:T(128)} %get-tuple-element.35.index_ref, f32[8,16]{1,0:T(8,128)} %get-tuple-element.36.decay_ref, bf16[8,16,128,128]{3,2,1,0:T(8,128)(2,1)} %state_ref.5, bf16[2,16,128,128]{3,2,1,0:T(8,128)(2,1)} %get-tuple-element.37.one_ref, ...), custom_call_target="tpu_custom_call" | custom-call | flops 8388608 | bytes 8388608 | tf_op jit(solution)/shard_map/update_states/pallas_call | solution.py:429
  (9 shorter events, 0.1 us)
Async XLA Ops:
  0.6 76.8 %copy-start = (bf16[2048,128]{1,0:T(8,128)(2,1)S(1)}, bf16[2048,128]{1,0:T(8,128)(2,1)}, u32[]{:S(2)}) copy-start(bf16[2048,128]{1,0:T(8,128)(2,1)} %param.17) | copy-start | bytes 1572868
  6.1 28.2 %copy-start.8 = (bf16[2,4,128,128]{3,2,1,0:T(8,128)(2,1)S(1)}, bf16[2,4,128,128]{3,2,1,0:T(8,128)(2,1)}, u32[]{:S(2)}) copy-start(bf16[2,4,128,128]{3,2,1,0:T(8,128)(2,1)} %get-tuple-element.38) | copy-start | bytes 786436
  6.1 29.1 %copy-start.7 = (bf16[2,4,128,128]{3,2,1,0:T(8,128)(2,1)S(1)}, bf16[2,4,128,128]{3,2,1,0:T(8,128)(2,1)}, u32[]{:S(2)}) copy-start(bf16[2,4,128,128]{3,2,1,0:T(8,128)(2,1)} %get-tuple-element.39) | copy-start | bytes 786436
  6.1 29.4 %copy-start.5 = (s32[1,4,32]{2,1,0:T(4,128)S(1)}, s32[1,4,32]{2,1,0:T(4,128)}, u32[]{:S(2)}) copy-start(s32[1,4,32]{2,1,0:T(4,128)} %list_ref.1) | copy-start | bytes 1540
  6.1 31.2 %copy-start.4 = (f32[16,128]{1,0:T(8,128)S(1)}, f32[16,128]{1,0:T(8,128)}, u32[]{:S(2)}) copy-start(f32[16,128]{1,0:T(8,128)} %param.14) | copy-start | bytes 24580
  6.1 31.3 %copy-start.6 = (f32[16]{0:T(128)S(1)}, f32[16]{0:T(128)}, u32[]{:S(2)}) copy-start(f32[16]{0:T(128)} %bias_ref.1) | copy-start | bytes 196
  34.3 43.2 %copy-start.3 = (bf16[128,128]{1,0:T(8,128)(2,1)S(1)}, bf16[128,128]{1,0:T(8,128)(2,1)}, u32[]{:S(2)}) copy-start(bf16[128,128]{1,0:T(8,128)(2,1)} %get-tuple-element.23.in_ref) | copy-start | bytes 98308
  34.3 45.4 %collective-permute-start = (bf16[2,4,128,128]{3,2,1,0:T(8,128)(2,1)S(1)}, bf16[2,4,128,128]{3,2,1,0:T(8,128)(2,1)S(1)}, u32[]{:S(2)}, u32[]{:S(2)}) collective-permute-start(bf16[2,4,128,128]{3,2,1,0:T(8,128)(2,1)S(1)} %copy-done.8), channel_id=1, source_target_pairs={{0,2},{1,3},{2,0},{3,1},{4,6},{5,7},{6,4},{7,5},{8,10},{9,11},{10,... | collective-permute-start | bytes 786440 | tf_op jit(solution)/shard_map/ppermute | solution.py:451
  35.2 44.5 %collective-permute-start.1 = (bf16[2,4,128,128]{3,2,1,0:T(8,128)(2,1)S(1)}, bf16[2,4,128,128]{3,2,1,0:T(8,128)(2,1)S(1)}, u32[]{:S(2)}, u32[]{:S(2)}) collective-permute-start(bf16[2,4,128,128]{3,2,1,0:T(8,128)(2,1)S(1)} %copy-done.7), channel_id=1, source_target_pairs={{0,3},{1,2},{2,1},{3,0},{4,7},{5,6},{6,5},{7,4},{8,11},{9,10},{10,... | collective-permute-start | bytes 786440 | tf_op jit(solution)/shard_map/ppermute | solution.py:451
  79.7 0.7 copy-start.1
  79.7 0.8 copy-start.2

commit v4 on v3

--- a/solution.py
+++ b/solution.py
@@ -9,7 +9,7 @@
 from jax.sharding import PartitionSpec as P
 
 CAP = 2
-AHEAD, BEHIND, MIDDLE = 2, 3, 4
+AHEAD, BEHIND, MIDDLE = 3, 2, 7
 ANY = pl.BlockSpec(memory_space=pl.ANY)
 VM = pl.BlockSpec(memory_space=pltpu.VMEM)
 SM = pl.BlockSpec(memory_space=pltpu.SMEM)
@@ -410,7 +410,7 @@
 
     def step(row, carry):
         pltpu.make_async_copy(state_ref.at[0], old.at[row], in_sem.at[row]).wait()
-        columns = unit_ref[row]
+        columns = jnp.transpose(unit_ref[row])
         values = value_ref[row]
         for head in range(heads):
             fresh = columns[:, head : head + 1] * values[head : head + 1, :]
@@ -514,7 +514,7 @@
     logit = jnp.sum(keys * gate_weight[:, None, :], axis=-1) / math.sqrt(head_size)
     decay = jax.nn.sigmoid(logit + gate_bias[:, None]).T
     unit = keys * lax.rsqrt(jnp.sum(keys * keys, axis=-1, keepdims=True) + 1e-06)
-    unit = jnp.transpose(unit, (1, 2, 0))
+    unit = jnp.swapaxes(unit, 0, 1)
     normed, pick, decay, unit, values, kind, index = lax.optimization_barrier(
         (normed, pick, decay, unit, values, kind, index)
     )

time: 87.2 us -> 78.6 us (0.901)
  Pallas kernels: 75.5 us -> 66.3 us
    pallas_call x1, Pallas kernels: 28.9 us -> 21.7 us  [spread_normed(): pl.pallas_call(functools.partial(normed_kernel, count, first, heads), out...]
    pallas_call x1, Pallas kernels: 28.2 us -> 25.5 us  [inputs(): pl.pallas_call(functools.partial(inputs_kernel, count, beams, split), out...]
    optimization_barrier x1 -> x0, local copies, waits for them, and re-layouts: 1 us -> none  [fast(): lax.optimization_barrier((normed, pick, decay, unit, values, kind, index))]
  transfers between devices with their start and end apart: 2 -> 2, of which waited for: 0 -> 0; matrix products, arithmetic and copies ran while one was open for 10% -> 10% of each run, Pallas kernels for 41% -> 37%
where the time goes in v4:
time: 78.6 us; the launch traced here: 78 us
  Pallas kernels  66.3 us (84%)
  other arithmetic  4.62 us (6%)
  matrix products  2.29 us (3%)
  local copies, waits for them, and re-layouts  2.22 us (3%)
  starting transfers between devices  1.8 us (2%)
  between operations  0.81 us (1%)
    pallas_call x1, Pallas kernels, inputs(): pl.pallas_call(functools.partial(inputs_kernel, count, beams, split), out...  25.5 us
    pallas_call x1, Pallas kernels, spread_normed(): pl.pallas_call(functools.partial(normed_kernel, count, first, heads), out...  21.7 us
    pallas_call x1, Pallas kernels, read(): pl.pallas_call(functools.partial(read_kernel, head_size), grid=(heads //...  6.75 us
    pallas_call x1, Pallas kernels, update(): pl.pallas_call(functools.partial(update_kernel, cuts), out_shape=jax.Shap...  6.66 us
    pallas_call x1, Pallas kernels, gather(): pl.pallas_call(functools.partial(gather_kernel, middle), out_shape=(jax.S...  5.61 us
    dot_general x1, matrix products, fast(): jnp.dot(ordered.astype(jnp.bfloat16), out_weight, preferred_element_type=...  2.29 us
    ppermute x2, starting transfers between devices, swap(): lax.ppermute(block, 'rows', [(low, low ^ partner) for low in range(count)])  1.8 us
  transfers between devices with their start and end apart: 2, of which 0 were waited for; matrix products, arithmetic and copies ran while one was open for 10% of the time, Pallas kernels for 37%

profile of v4, /device:TPU:0, one launch (start us, length us, event | category | flops | bytes accessed | tf_op | source)
XLA Modules:
  0.0 78.0 jit_solution(6020173685224340165)
XLA Ops:
  0.6 0.0 copy-start
  0.6 5.6 %gather_rows.1 = (bf16[2,16,128,128]{3,2,1,0:T(8,128)(2,1)}, bf16[4,16,128,128]{3,2,1,0:T(8,128)(2,1)}, bf16[2,7,128,128]{3,2,1,0:T(8,128)(2,1)}, bf16[2,7,128,128]{3,2,1,0:T(8,128)(2,1)}, bf16[128,128]{1,0:T(8,128)(2,1)}) custom-call(s32[1,4,32]{2,1,0:T(4,128)} %list_ref.1, s32[1,128]{1,0:T(1,128)} %tok_ref.1, bf16[8,16,128,128]{3,2,1,0:T(8,128)(2,1)} %state_ref.5, ...), custom_call_target="tpu_custom_call" | custom-call | bytes 6291456 | tf_op jit(solution)/shard_map/gather_rows/pallas_call | solution.py:77
  6.3 0.0 copy-start.8
  6.3 0.0 copy-start.7
  6.3 0.0 copy-start.5
  6.3 0.0 copy-start.4
  6.3 0.0 copy-start.6
  6.3 25.5 %spread_inputs.1 = (bf16[512,384]{1,0:T(8,128)(2,1)}, bf16[4,5,128,128]{3,2,1,0:T(8,128)(2,1)}, bf16[2,16,128,128]{3,2,1,0:T(8,128)(2,1)}) custom-call(bf16[128,128]{1,0:T(8,128)(2,1)} %get-tuple-element.23.in_ref, bf16[3,2048,128]{2,1,0:T(8,128)(2,1)} %bitcast.56, bf16[4,16,128,128]{3,2,1,0:T(8,128)(2,1)} %get-tuple-element.26.far_ref, ...), custom_call_target="tpu_custom_call" | custom-call | tf_op jit(solution)/shard_map/spread_inputs/pallas_call | solution.py:257
  31.8 0.0 copy-start.3
  31.8 0.0 copy-done.8
  31.8 1.4 %collective-permute-start = (bf16[2,7,128,128]{3,2,1,0:T(8,128)(2,1)S(1)}, bf16[2,7,128,128]{3,2,1,0:T(8,128)(2,1)S(1)}, u32[]{:S(2)}, u32[]{:S(2)}) collective-permute-start(bf16[2,7,128,128]{3,2,1,0:T(8,128)(2,1)S(1)} %copy-done.8), channel_id=1, source_target_pairs={{0,2},{1,3},{2,0},{3,1},{4,6},{5,7},{6,4},{7,5},{8,10},{9,11},{10,... | collective-permute-start | bytes 1376264 | tf_op jit(solution)/shard_map/ppermute | solution.py:451
  33.2 0.0 copy-done.7
  33.2 0.4 collective-permute-start.1
  33.6 0.0 copy-done.5
  33.7 0.1 broadcast_in_dim.16
  33.8 0.1 xor.14
  33.9 0.1 eq.92
  34.0 0.4 convert_reduce_fusion
  34.4 0.1 reduce_sum.30
  34.5 0.1 multiply_add_fusion
  34.6 0.1 eq.100
  34.7 0.8 %constant_dynamic-slice_fusion.1 = (bf16[16,8,128]{2,1,0:T(8,128)(2,1)S(1)}, bf16[16,8,128]{2,1,0:T(8,128)(2,1)S(1)}) fusion(bf16[16,32,384]{2,1,0:T(8,128)(2,1)} %bitcast.57, s32[]{:T(128)S(6)} %select_n.83, s32[]{:T(128)S(6)} %add.118, s32[]{:T(128)S(6)} %add.117), kind=kLoop, calls=%fused_computation.51 | loop fusion | bytes 131084 | tf_op jit(solution)/shard_map/slice | solution.py:513
  35.5 0.6 convert_bitcast_fusion.value_ref
  36.1 0.1 fusion.4
  36.2 0.6 fusion.11.slot_ref
  36.8 0.7 fusion.9.owner_ref
  37.4 0.0 copy-done.4
  37.5 0.1 fusion.6
  37.6 0.0 copy-done.6
  37.6 0.6 divide_bitcast_fusion
  38.2 0.7 bitcast_select_fusion
  38.9 6.8 %read_heads.1.in_ref = bf16[16,2048]{1,0:T(8,128)(2,1)} custom-call(f32[16]{0:T(128)} %bias_ref.1, bf16[16,32,384]{2,1,0:T(8,128)(2,1)} %bitcast.58, bf16[8,16,128,128]{3,2,1,0:T(8,128)(2,1)} %state_ref.5, f32[16,1,128]{2,1,0:T(1,128)} %bitcast.59, f32[16,1,128]{2,1,0:T(1,128)} %bitcast.64, f32[32,8]{1,0:T(8,128)} %fusion.9.owner_ref, ...), custom_call_target="tpu_custom_call" | custom-call | flops 134217728 | bytes 4194304 | tf_op jit(solution)/shard_map/read_heads/pallas_call | solution.py:349
  45.6 0.7 fusion.7.unit_ref
  46.3 21.7 %spread_normed.1 = (bf16[256,2048]{1,0:T(8,128)(2,1)}, bf16[4,4,128,128]{3,2,1,0:T(8,128)(2,1)}) custom-call(bf16[16,2048]{1,0:T(8,128)(2,1)} %read_heads.1.in_ref, bf16[4,16,128,128]{3,2,1,0:T(8,128)(2,1)} %get-tuple-element.26.far_ref), custom_call_target="tpu_custom_call" | custom-call | tf_op jit(solution)/shard_map/spread_normed/pallas_call | solution.py:297
  68.1 0.0 copy-done
  68.1 0.0 copy-done.3
  68.1 2.3 %fusion.3 = bf16[1,128,128]{2,1,0:T(8,128)(2,1)} fusion(bf16[2048,128]{1,0:T(8,128)(2,1)S(1)} %copy-done, bf16[128,256]{1,0:T(8,128)(2,1)S(1)} %fusion.4, bf16[256,2048]{1,0:T(8,128)(2,1)} %get-tuple-element.33, bf16[128,128]{1,0:T(8,128)(2,1)S(1)} %copy-done.3), kind=kOutput, calls=%fused_computation.4 | convolution fusion | flops 201637888 | bytes 1703936 | tf_op jit(solution)/shard_map/dot_general | solution.py:523
  70.4 0.0 collective-permute-done.two_ref
  70.4 0.0 copy-start.1
  70.4 0.0 collective-permute-done.1.three_ref
  70.4 0.0 copy-start.2
  70.4 0.8 copy-done.1
  71.2 0.2 copy-done.2
  71.3 6.7 %update_states.1 = bf16[8,16,128,128]{3,2,1,0:T(8,128)(2,1)} custom-call(s32[8]{0:T(128)} %get-tuple-element.34.kind_ref, s32[8]{0:T(128)} %get-tuple-element.35.index_ref, f32[8,16]{1,0:T(8,128)} %get-tuple-element.36.decay_ref, bf16[8,16,128,128]{3,2,1,0:T(8,128)(2,1)} %state_ref.5, bf16[2,16,128,128]{3,2,1,0:T(8,128)(2,1)} %get-tuple-element.37.one_ref, ...), custom_call_target="tpu_custom_call" | custom-call | flops 8388608 | bytes 8388608 | tf_op jit(solution)/shard_map/update_states/pallas_call | solution.py:429
  (9 shorter events, 0.1 us)
Async XLA Ops:
  0.6 67.4 %copy-start = (bf16[2048,128]{1,0:T(8,128)(2,1)S(1)}, bf16[2048,128]{1,0:T(8,128)(2,1)}, u32[]{:S(2)}) copy-start(bf16[2048,128]{1,0:T(8,128)(2,1)} %param.17) | copy-start | bytes 1572868
  6.3 25.6 %copy-start.8 = (bf16[2,7,128,128]{3,2,1,0:T(8,128)(2,1)S(1)}, bf16[2,7,128,128]{3,2,1,0:T(8,128)(2,1)}, u32[]{:S(2)}) copy-start(bf16[2,7,128,128]{3,2,1,0:T(8,128)(2,1)} %get-tuple-element.38) | copy-start | bytes 1376260
  6.3 27.0 %copy-start.7 = (bf16[2,7,128,128]{3,2,1,0:T(8,128)(2,1)S(1)}, bf16[2,7,128,128]{3,2,1,0:T(8,128)(2,1)}, u32[]{:S(2)}) copy-start(bf16[2,7,128,128]{3,2,1,0:T(8,128)(2,1)} %get-tuple-element.39) | copy-start | bytes 1376260
  6.3 27.4 %copy-start.5 = (s32[1,4,32]{2,1,0:T(4,128)S(1)}, s32[1,4,32]{2,1,0:T(4,128)}, u32[]{:S(2)}) copy-start(s32[1,4,32]{2,1,0:T(4,128)} %list_ref.1) | copy-start | bytes 1540
  6.3 31.2 %copy-start.4 = (f32[16,128]{1,0:T(8,128)S(1)}, f32[16,128]{1,0:T(8,128)}, u32[]{:S(2)}) copy-start(f32[16,128]{1,0:T(8,128)} %param.14) | copy-start | bytes 24580
  6.3 31.3 %copy-start.6 = (f32[16]{0:T(128)S(1)}, f32[16]{0:T(128)}, u32[]{:S(2)}) copy-start(f32[16]{0:T(128)} %bias_ref.1) | copy-start | bytes 196
  31.8 36.3 %copy-start.3 = (bf16[128,128]{1,0:T(8,128)(2,1)S(1)}, bf16[128,128]{1,0:T(8,128)(2,1)}, u32[]{:S(2)}) copy-start(bf16[128,128]{1,0:T(8,128)(2,1)} %get-tuple-element.23.in_ref) | copy-start | bytes 98308
  31.8 38.5 %collective-permute-start = (bf16[2,7,128,128]{3,2,1,0:T(8,128)(2,1)S(1)}, bf16[2,7,128,128]{3,2,1,0:T(8,128)(2,1)S(1)}, u32[]{:S(2)}, u32[]{:S(2)}) collective-permute-start(bf16[2,7,128,128]{3,2,1,0:T(8,128)(2,1)S(1)} %copy-done.8), channel_id=1, source_target_pairs={{0,2},{1,3},{2,0},{3,1},{4,6},{5,7},{6,4},{7,5},{8,10},{9,11},{10,... | collective-permute-start | bytes 1376264 | tf_op jit(solution)/shard_map/ppermute | solution.py:451
  33.2 37.2 %collective-permute-start.1 = (bf16[2,7,128,128]{3,2,1,0:T(8,128)(2,1)S(1)}, bf16[2,7,128,128]{3,2,1,0:T(8,128)(2,1)S(1)}, u32[]{:S(2)}, u32[]{:S(2)}) collective-permute-start(bf16[2,7,128,128]{3,2,1,0:T(8,128)(2,1)S(1)} %copy-done.7), channel_id=1, source_target_pairs={{0,3},{1,2},{2,1},{3,0},{4,7},{5,6},{6,5},{7,4},{8,11},{9,10},{10,... | collective-permute-start | bytes 1376264 | tf_op jit(solution)/shard_map/ppermute | solution.py:451
  70.4 0.8 %copy-start.1 = (bf16[2,7,128,128]{3,2,1,0:T(8,128)(2,1)}, bf16[2,7,128,128]{3,2,1,0:T(8,128)(2,1)S(1)}, u32[]{:S(2)}) copy-start(bf16[2,7,128,128]{3,2,1,0:T(8,128)(2,1)S(1)} %collective-permute-done.two_ref) | copy-start | bytes 1376260
  70.4 1.0 %copy-start.2 = (bf16[2,7,128,128]{3,2,1,0:T(8,128)(2,1)}, bf16[2,7,128,128]{3,2,1,0:T(8,128)(2,1)S(1)}, u32[]{:S(2)}) copy-start(bf16[2,7,128,128]{3,2,1,0:T(8,128)(2,1)S(1)} %collective-permute-done.1.three_ref) | copy-start | bytes 1376260
